TPU v7x, 32 devices: a whole 2x2x4 slice. The times are simulated.
32 devices in a mesh: role: 2 (over y), proto: 8 (over z, x), crop: 2 (over core).
Axes of the slice: x: 2, y: 2, z: 4, core: 2. Of those that a mesh axis runs over, the one named last changes fastest.
Arguments:
- embeddings: bfloat16 [2, 1024, 512], P('role', 'crop'), may hold values from -1 to 1, as said below
- weights: bfloat16 [2, 512, 262144], P('role', None, 'proto'), may hold values from -1 to 1, as said below
Outputs:
- weight_grad: bfloat16 [2, 2, 128, 262144], P('crop', 'role', None, 'proto')
- embed_grad: bfloat16 [2, 512, 512], P('crop', 'proto', 'role')
Inputs may be any that keep to these rules, and one draw needn't show every extreme that they name: `embeddings`: each crop's row has unit Euclidean length before rounding to bfloat16. `weights`: each prototype column has unit Euclidean length before rounding to bfloat16.
All inputs are finite; a program needn't handle non-finite values.
Results may differ from a plain program's by a relative error of at most 0.001.
The roundings to bfloat16 on the way count: a program that leaves them out, or rounds other values in their place, can miss the bound.
Values may be sent and summed in bfloat16 or wider, within the bound.
No kernel may reach another device: no remote copies, remote signals or barrier semaphores. Data moves between devices by JAX's collectives and lax.ppermute only.
A program may use at most 256 MiB of HBM per device.

v0:
```python
import functools
import math

import jax
import jax.numpy as jnp
from jax import lax
from jax.experimental import pallas as pl
from jax.experimental.pallas import tpu as pltpu
from jax.sharding import PartitionSpec as P


ITERS = 3
LOG2E = 1.4426950408889634
SHARES = (4, 4, 5, 3)
CHUNKS = len(SHARES)
GRAD_ORDER = (1, 2, 0, 3)
ROWS = 256
NT = (((1,), (1,)), ((), ()))


def whole(shape):
    return pl.BlockSpec(shape, lambda *_: (0,) * len(shape), pipeline_mode=pl.Buffered(1))


def cost(flops, bytes_accessed, transcendentals):
    return pl.CostEstimate(
        flops=flops, bytes_accessed=bytes_accessed, transcendentals=transcendentals
    )


def tile_width(quarter_width):
    return 512 if quarter_width % 8192 == 0 else 128


def chunk_tiles(quarter_width):
    tiles = quarter_width // tile_width(quarter_width)
    edges = [-(-tiles * sum(SHARES[:n]) // sum(SHARES)) for n in range(CHUNKS + 1)]
    return [(begin, end - begin) for begin, end in zip(edges, edges[1:])]


def lane_tiles(value, width):
    return jnp.concatenate([value] * (width // value.shape[1]), axis=1)


def copy_body(places, source, target):
    target[...] = source[...]


def columns_of(places, matrix, chunk):
    depth = matrix.shape[0]
    quarter_width = matrix.shape[1] // 4
    tile = tile_width(quarter_width)
    tiles = quarter_width // tile
    begin, count = chunk_tiles(quarter_width)[chunk]
    width = count * tile
    return pl.pallas_call(
        copy_body,
        out_shape=jax.ShapeDtypeStruct((depth, width), matrix.dtype),
        grid_spec=pltpu.PrefetchScalarGridSpec(
            num_scalar_prefetch=1,
            grid=(count,),
            in_specs=[
                pl.BlockSpec(
                    (depth, tile), lambda t, places: (0, places[2] * tiles + begin + t)
                )
            ],
            out_specs=pl.BlockSpec((depth, tile), lambda t, places: (0, t)),
        ),
        cost_estimate=cost(0, 4 * depth * width, 0),
        name="columns_of",
    )(places, matrix)


def reciprocal_rows(parts, crops):
    total = parts[0][...]
    for part in parts[1:]:
        total = total + part[...]
    return jnp.transpose(jnp.broadcast_to(1.0 / total, (128, crops)))


def pass_body(first, nparts, tiles, places, scale, embed, weight, *refs):
    parts, refs = refs[:nparts], refs[nparts:]
    row_sums, own_factor, partner_factor = refs[:3]
    sent = refs[3:-3] if first else ()
    kept, sums, row_scale = refs[-3:]
    step = pl.program_id(0)
    crops = embed.shape[0]
    width = weight.shape[1]

    @pl.when(step == 0)
    def _():
        sums[...] = jnp.zeros_like(sums)
        if not first:
            row_scale[...] = reciprocal_rows(parts, crops)

    block = weight[...]
    total = jnp.zeros((8, width), jnp.float32)
    for start in range(0, crops, ROWS):
        rows = pl.ds(start, ROWS)
        scores = jnp.dot(embed[rows, :], block, preferred_element_type=jnp.float32)
        powers = jnp.exp2(scores * scale[0])
        kept[rows, :] = powers
        if not first:
            powers = powers * lane_tiles(row_scale[rows, :], width)
        total += jnp.sum(powers.reshape(ROWS // 8, 8, width), axis=0)
    column_sum = jnp.sum(total, axis=0, keepdims=True)
    factor = jnp.where(places[0] == 1, 1.0, 1.0 / column_sum)
    owned = step // tiles == places[0]

    @pl.when(owned)
    def _():
        own_factor[...] = factor

    @pl.when(jnp.logical_not(owned))
    def _():
        partner_factor[...] = factor

    here = lax.rem(step, tiles)
    for (begin, count), piece in zip(chunk_tiles(tiles * width)[1:], sent):

        @pl.when(jnp.logical_not(owned) & (here >= begin) & (here < begin + count))
        def _(piece=piece):
            piece[...] = block

    for start in range(0, crops, ROWS):
        rows = pl.ds(start, ROWS)
        part = kept[rows, :] * factor
        folded = part[:, :128]
        for lane in range(128, width, 128):
            folded += part[:, lane : lane + 128]
        sums[rows, :] += folded

    @pl.when(step == pl.num_programs(0) - 1)
    def _():
        ones = jnp.ones((8, 128), jnp.float32)
        row_sums[...] = lax.dot_general(
            ones,
            sums[...],
            NT,
            precision=lax.Precision.HIGHEST,
            preferred_element_type=jnp.float32,
        )[:1]


def sinkhorn_pass(places, scale, embed, weight, parts):
    crops, depth = embed.shape
    quarter_width = weight.shape[1] // 4
    tile = tile_width(quarter_width)
    tiles = quarter_width // tile
    first = not parts

    def owner_spec(partner):
        def index(t, places):
            begin = tiles * (1 - places[0] if partner else places[0])
            return (0, jnp.clip(t - begin, 0, tiles - 1))

        return pl.BlockSpec((1, tile), index)

    def sent_spec(begin, count):
        def index(t, places):
            return (0, jnp.clip(t - tiles * (1 - places[0]) - begin, 0, count - 1))

        return pl.BlockSpec((depth, tile), index)

    sent = chunk_tiles(quarter_width)[1:] if first else ()
    factor_shape = jax.ShapeDtypeStruct((1, quarter_width), jnp.float32)
    return pl.pallas_call(
        functools.partial(pass_body, first, len(parts), tiles),
        out_shape=[
            jax.ShapeDtypeStruct((1, crops), jnp.float32),
            factor_shape,
            factor_shape,
            *[jax.ShapeDtypeStruct((depth, count * tile), weight.dtype) for _, count in sent],
        ],
        grid_spec=pltpu.PrefetchScalarGridSpec(
            num_scalar_prefetch=1,
            grid=(2 * tiles,),
            in_specs=[
                pl.BlockSpec(memory_space=pltpu.SMEM),
                whole((crops, depth)),
                pl.BlockSpec((depth, tile), lambda t, places: (0, places[3] * 2 * tiles + t)),
                *[pl.BlockSpec(memory_space=pltpu.VMEM) for _ in parts],
            ],
            out_specs=[
                whole((1, crops)),
                owner_spec(False),
                owner_spec(True),
                *[sent_spec(begin, count) for begin, count in sent],
            ],
            scratch_shapes=[
                pltpu.VMEM((crops, tile), jnp.float32),
                pltpu.VMEM((crops, 128), jnp.float32),
                pltpu.VMEM((crops, 128), jnp.float32),
            ],
        ),
        cost_estimate=cost(
            4 * crops * depth * quarter_width, 4 * depth * quarter_width, 2 * crops * quarter_width
        ),
        name="sinkhorn_pass",
    )(places, scale, embed, weight, *parts)


def scales_body(nparts, places, *refs):
    parts, (got_inverse, own_factor, got_factor) = refs[:nparts], refs[nparts : nparts + 3]
    row_scale, inverse_sum, column_scale = refs[nparts + 3 :]
    crops = got_inverse.shape[1]
    mine = reciprocal_rows(parts, crops)
    theirs = jnp.transpose(jnp.broadcast_to(got_inverse[...], (128, crops)))
    teaches = places[0] == 0
    row_scale[...] = jnp.where(teaches, mine, theirs)
    inverse_sum[...] = jnp.where(teaches, theirs, mine)
    column_scale[...] = jnp.where(teaches, own_factor[...], got_factor[...])


def final_scales(places, parts, got_inverse, own_factor, got_factor):
    crops = got_inverse.shape[1]
    rows = jax.ShapeDtypeStruct((crops, 128), jnp.float32)
    return pl.pallas_call(
        functools.partial(scales_body, len(parts)),
        out_shape=[rows, rows, jax.ShapeDtypeStruct(own_factor.shape, jnp.float32)],
        grid_spec=pltpu.PrefetchScalarGridSpec(
            num_scalar_prefetch=1,
            grid=(1,),
            in_specs=[pl.BlockSpec(memory_space=pltpu.VMEM)] * (len(parts) + 3),
            out_specs=[whole((crops, 128))] * 2 + [whole(own_factor.shape)],
        ),
        cost_estimate=cost(0, 8 * crops * 128, 0),
        name="final_scales",
    )(places, *parts, got_inverse, own_factor, got_factor)


def grads_body(
    places,
    teacher_embed,
    student_embed,
    turned,
    own,
    arrived,
    row_scale,
    inverse_sum,
    column_scale,
    embed_start,
    kept_piece,
    crop_piece,
    role_piece,
    diagonal_piece,
    embed_total,
    logit_grads,
):
    step = pl.program_id(0)
    crops = teacher_embed.shape[0]
    width = own.shape[1]
    quarter = turned.shape[0] // 4

    @pl.when(step == 0)
    def _():
        embed_total[...] = embed_start[...]

    def tile(teacher, student):
        teacher_block = teacher[...]
        student_block = student[...]
        factor = column_scale[...]
        for start in range(0, crops, ROWS):
            rows = pl.ds(start, ROWS)
            teacher_scores = jnp.dot(
                teacher_embed[rows, :], teacher_block, preferred_element_type=jnp.float32
            )
            student_scores = jnp.dot(
                student_embed[rows, :], student_block, preferred_element_type=jnp.float32
            )
            targets = (
                jnp.exp2(teacher_scores * (LOG2E / 0.07))
                * factor
                * lane_tiles(row_scale[rows, :], width)
            ).astype(jnp.bfloat16)
            probs = jnp.exp2(student_scores * (LOG2E / 0.1)) * lane_tiles(
                inverse_sum[rows, :], width
            )
            grads = ((probs - targets.astype(jnp.float32)) * 10.0).astype(jnp.bfloat16)
            logit_grads[rows, :] = grads
            embed_total[rows, :] += lax.dot_general(
                grads, student_block, NT, preferred_element_type=jnp.float32
            )
        pieces = (kept_piece, crop_piece, role_piece, diagonal_piece)
        for place, piece in enumerate(pieces):
            piece[...] = jnp.dot(
                turned[pl.ds(place * quarter, quarter), :],
                logit_grads[...],
                preferred_element_type=jnp.float32,
            ).astype(piece.dtype)

    @pl.when(places[0] == 0)
    def _():
        tile(own, arrived)

    @pl.when(places[0] == 1)
    def _():
        tile(arrived, own)


def gradients(places, chunk, embeds, turned, own, arrived, scales, column_scale, embed_start):
    crops, depth = embeds[0].shape
    width = arrived.shape[1]
    quarter_width = own.shape[1] // 4
    tile = tile_width(quarter_width)
    tiles = quarter_width // tile
    begin, count = chunk_tiles(quarter_width)[chunk]
    quarter = depth // 4
    piece = jax.ShapeDtypeStruct((quarter, width), jnp.bfloat16)
    piece_spec = pl.BlockSpec((quarter, tile), lambda t, places: (0, t))
    return pl.pallas_call(
        grads_body,
        out_shape=(piece,) * 4 + (jax.ShapeDtypeStruct((crops, depth), jnp.float32),),
        grid_spec=pltpu.PrefetchScalarGridSpec(
            num_scalar_prefetch=1,
            grid=(count,),
            in_specs=[
                whole((crops, depth)),
                whole((crops, depth)),
                whole((depth, crops)),
                pl.BlockSpec(
                    (depth, tile),
                    lambda t, places: (0, places[1] * tiles + begin + t),
                ),
                pl.BlockSpec((depth, tile), lambda t, places: (0, t)),
                whole((crops, 128)),
                whole((crops, 128)),
                pl.BlockSpec((1, tile), lambda t, places: (0, begin + t)),
                whole((crops, depth)),
            ],
            out_specs=[piece_spec] * 4 + [whole((crops, depth))],
            scratch_shapes=[pltpu.VMEM((crops, tile), jnp.bfloat16)],
        ),
        cost_estimate=cost(
            8 * crops * depth * width, 6 * depth * width + 8 * crops * depth, 2 * crops * width
        ),
        name="gradients",
    )(
        places,
        *embeds,
        turned,
        own,
        arrived,
        *scales,
        column_scale,
        embed_start,
    )


def place_body(places, *refs):
    pieces, after = refs[:4], refs[-1]
    width = after.shape[1]
    step = pl.program_id(1)
    for place, piece in enumerate(pieces):

        @pl.when(pl.program_id(0) == place)
        def _(piece=piece):
            after[...] = piece[:, pl.ds(pl.multiple_of(step * width, width), width)]


def placed_pieces(places, chunk, pieces, before, block_width):
    rows, width = pieces[0].shape
    tile = tile_width(block_width // 4)
    tiles = block_width // 4 // tile
    begin, count = chunk_tiles(block_width // 4)[chunk]
    group = math.gcd(math.gcd(begin, count), tiles)
    operands = [places, *pieces] + ([] if before is None else [before])
    specs = [pl.BlockSpec(memory_space=pltpu.VMEM)] * 4
    if before is not None:
        specs = specs + [pl.BlockSpec(memory_space=pl.ANY)]
    return pl.pallas_call(
        place_body,
        out_shape=jax.ShapeDtypeStruct((rows, block_width), pieces[0].dtype),
        grid_spec=pltpu.PrefetchScalarGridSpec(
            num_scalar_prefetch=1,
            grid=(4, count // group),
            in_specs=specs,
            out_specs=pl.BlockSpec(
                (rows, group * tile),
                lambda p, t, places: (0, (places[4 + p] * tiles + begin) // group + t),
            ),
        ),
        input_output_aliases={} if before is None else {5: 0},
        cost_estimate=cost(0, 16 * rows * width, 0),
        name="placed_pieces",
    )(*operands)


def swapped(value, *axes):
    if axes == ("role", "crop"):
        return lax.ppermute(value, axes, [(0, 3), (1, 2), (2, 1), (3, 0)])
    return lax.ppermute(value, axes[0], [(0, 1), (1, 0)])


def summands(value):
    axes = ("proto", "crop")
    count = lax.axis_size("proto") * lax.axis_size("crop")
    if count & (count - 1):
        return [lax.psum(value, axes)]
    parts = [value]
    stride = 1
    while stride < count:
        if stride > 1:
            parts = [functools.reduce(jnp.add, parts)]
        masks = [stride * k for k in (1, 2, 3) if stride * k < count]
        for mask in masks:
            pairs = [(place, place ^ mask) for place in range(count)]
            parts.append(lax.ppermute(parts[0], axes, pairs))
        stride *= 4
    return parts


def halving_masks(axis):
    count = lax.axis_size(axis)
    return [1 << bit for bit in range(count.bit_length() - 1)]


def is_power_of_two(count):
    return count & (count - 1) == 0


def flipped(value, axis, mask):
    return lax.ppermute(value, axis, [(p, p ^ mask) for p in range(lax.axis_size(axis))])


def bit_of(place, mask):
    return jnp.where((place & mask) != 0, 1, 0)


def scattered(value):
    count = lax.axis_size("proto")
    if not is_power_of_two(count):
        return lax.psum_scatter(value, ("crop", "proto"), scatter_dimension=0, tiled=True)
    width = value.shape[1]
    rows = value.shape[0] // 2 // count
    steps = [("crop", 1)] + [("proto", mask) for mask in halving_masks("proto")]
    for axis, mask in steps:
        bit = bit_of(lax.axis_index(axis), mask)
        low = value.shape[0] // 2 if axis == "crop" else rows
        halves = value.reshape(-1, 2, low, width)
        theirs = lax.dynamic_index_in_dim(halves, 1 - bit, 1, keepdims=False)
        mine = lax.dynamic_index_in_dim(halves, bit, 1, keepdims=False)
        got = flipped(theirs.reshape(-1, width), axis, mask)
        value = mine.reshape(-1, width) + got
    return value


def joined(mine, other, bit):
    return jnp.concatenate(
        [jnp.where(bit == 0, mine, other), jnp.where(bit == 0, other, mine)], axis=0
    )


def step(embeddings, weights):
    role_place = lax.axis_index("role")
    crop_place = lax.axis_index("crop")
    own_embed = embeddings[0]
    own_weight = weights[0]
    crops = 2 * own_embed.shape[0]
    depth = own_embed.shape[1]
    block_width = own_weight.shape[1]
    teaches = role_place == 0

    own_quarter = 2 * crop_place + role_place
    partner_quarter = 2 * crop_place + 1 - role_place
    order = [own_quarter, own_quarter ^ 2, own_quarter ^ 1, own_quarter ^ 3]
    places = jnp.stack([role_place, own_quarter, partner_quarter, crop_place] + order).astype(
        jnp.int32
    )

    first_columns = columns_of(places, own_weight, 0)
    arrived = [swapped(first_columns, "role")]
    crop_embed = swapped(own_embed, "crop")
    proto_place = lax.axis_index("proto")
    spread = is_power_of_two(lax.axis_size("proto"))
    masks = halving_masks("proto") if spread else []
    part_rows = own_embed.shape[0] // lax.axis_size("proto") if spread else own_embed.shape[0]
    part_start = part_rows * proto_place if spread else 0
    role_embed = swapped(lax.dynamic_slice_in_dim(own_embed, part_start, part_rows), "role")
    got_embed = None
    if masks:
        got_embed = flipped(role_embed, "proto", masks[0])
    own_all = joined(own_embed, crop_embed, crop_place)

    scale = jnp.where(teaches, LOG2E / 0.07, LOG2E / 0.1).astype(jnp.float32).reshape(1)
    parts = []
    for iteration in range(ITERS):
        row_sums, own_factor, partner_factor, *columns = sinkhorn_pass(
            places, scale, own_all, own_weight, parts
        )
        if iteration == 0:
            for chunk in range(1, CHUNKS):
                arrived.append(swapped(columns[chunk - 1], "role"))
        parts = summands(row_sums)
        for place, mask in enumerate(masks):
            if min(place, ITERS - 1) != iteration:
                continue
            role_embed, got_embed, _ = lax.optimization_barrier((role_embed, got_embed, row_sums))
            role_embed = joined(role_embed, got_embed, bit_of(proto_place, mask))
            if place + 1 < len(masks):
                got_embed = flipped(role_embed, "proto", masks[place + 1])

    role_embed, own_all, _ = lax.optimization_barrier((role_embed, own_all, row_sums))
    diagonal_embed = swapped(role_embed, "crop")
    other_all = joined(role_embed, diagonal_embed, crop_place)
    embeds = (jnp.where(teaches, own_all, other_all), jnp.where(teaches, other_all, own_all))
    blocks = embeds[1].T.reshape(4, depth // 4, crops)
    turned = jnp.concatenate(
        [lax.dynamic_index_in_dim(blocks, place, 0, keepdims=False) for place in order], axis=0
    )

    got_factor = swapped(partner_factor, "role")
    inverse = 1.0 / functools.reduce(jnp.add, parts)
    got_inverse = swapped(inverse, "role")
    row_scale, inverse_sum, columns = final_scales(
        places, parts, got_inverse, own_factor, got_factor
    )

    embed_part = jnp.zeros((crops, depth), jnp.float32)
    result = None
    for chunk in GRAD_ORDER:
        kept_piece, crop_piece, role_piece, diagonal_piece, embed_part = gradients(
            places,
            chunk,
            embeds,
            turned,
            own_weight,
            arrived[chunk],
            (row_scale, inverse_sum),
            columns,
            embed_part,
        )
        diagonal_piece = swapped(diagonal_piece, "role", "crop")
        role_piece = swapped(role_piece, "role")
        crop_piece = swapped(crop_piece, "crop")
        pieces = (kept_piece, crop_piece, role_piece, diagonal_piece)
        result = placed_pieces(places, chunk, pieces, result, block_width)
    weight_block = result.reshape(1, 1, depth // 4, block_width)

    summed = scattered(embed_part)
    sides = summed.reshape(summed.shape[0], 2, depth // 2)
    theirs = lax.dynamic_index_in_dim(sides, 1 - role_place, 1, keepdims=False)
    mine = lax.dynamic_index_in_dim(sides, role_place, 1, keepdims=False)
    got_side = swapped(theirs, "role")
    embed_block = (mine + got_side).astype(jnp.bfloat16)[None]
    return (weight_block, embed_block)


def solution(mesh):
    placed = (P("role", "crop", None), P("role", None, "proto"))
    return jax.shard_map(
        step,
        mesh=mesh,
        in_specs=placed,
        out_specs=(P("crop", "role", None, "proto"), P("crop", "proto", "role")),
        check_vma=False,
    )
```

profile of v0, /device:TPU:0, one launch (start us, length us, event | category | flops | bytes accessed | tf_op | source)
XLA Modules:
  0.0 406.0 jit_solution(10050758412772203333)
XLA Ops:
  2.0 2.5 collective-permute-start
  5.2 2.1 collective-permute-done
  7.3 1.7 collective-permute-start.1
  11.3 37.3 %sinkhorn_pass.3 = (f32[1,1024]{1,0:T(1,128)}, f32[1,8192]{1,0:T(1,128)}, f32[1,8192]{1,0:T(1,128)}, bf16[512,2048]{1,0:T(8,128)(2,1)}, bf16[512,2560]{1,0:T(8,128)(2,1)}, /*index=5*/bf16[512,1536]{1,0:T(8,128)(2,1)}) custom-call(s32[8]{0:T(128)} %stack.32.places, f32[1]{0:T(128)} %bitcast.8.scale, bf16[1024,512]{1,0:T(8,128)(2,1)} %pad_maximum_fusion.embed, ...), custom_call_target="tpu_custom_call" | custom-call | flops 17179869184 | bytes 16777216 | tf_op jit(solution)/shard_map/sinkhorn_pass/pallas_call | solution.py:167
  53.2 3.7 collective-permute-start.9
  58.7 2.7 collective-permute-done.8.refs_2_
  62.5 35.3 %sinkhorn_pass.4 = (f32[1,1024]{1,0:T(1,128)}, f32[1,8192]{1,0:T(1,128)}, f32[1,8192]{1,0:T(1,128)}) custom-call(s32[8]{0:T(128)} %stack.32.places, f32[1]{0:T(128)} %bitcast.8.scale, bf16[1024,512]{1,0:T(8,128)(2,1)} %pad_maximum_fusion.embed, bf16[512,32768]{1,0:T(8,128)(2,1)} %bitcast.55, f32[1,1024]{1,0:T(1,128)} %copy-done.19, f32[1,1024]{1,0:T(1,128)} %copy-done.27, ...), custom_call_target="tpu_custom_call" | custom-call | flops 17179869184 | bytes 16777216 | tf_op jit(solution)/shard_map/sinkhorn_pass/pallas_call | solution.py:167
  103.4 2.2 collective-permute-start.16
  106.2 1.7 collective-permute-start.14
  111.7 35.3 %sinkhorn_pass.5 = (f32[1,1024]{1,0:T(1,128)}, f32[1,8192]{1,0:T(1,128)}, f32[1,8192]{1,0:T(1,128)}) custom-call(s32[8]{0:T(128)} %stack.32.places, f32[1]{0:T(128)} %bitcast.8.scale, bf16[1024,512]{1,0:T(8,128)(2,1)} %pad_maximum_fusion.embed, bf16[512,32768]{1,0:T(8,128)(2,1)} %bitcast.56, f32[1,1024]{1,0:T(1,128)} %copy-done.17, f32[1,1024]{1,0:T(1,128)} %copy-done.24, ...), custom_call_target="tpu_custom_call" | custom-call | flops 17179869184 | bytes 16777216 | tf_op jit(solution)/shard_map/sinkhorn_pass/pallas_call | solution.py:167
  152.0 1.7 collective-permute-start.24
  154.6 2.9 collective-permute-done.24.refs_3_
  159.1 2.0 collective-permute-done.22.refs_1_
  162.7 4.5 %columns_of.1 = bf16[512,2048]{1,0:T(8,128)(2,1)} custom-call(s32[8]{0:T(128)} %stack.32.places, bf16[512,32768]{1,0:T(8,128)(2,1)} %bitcast.57), custom_call_target="tpu_custom_call" | custom-call | bytes 4194304 | tf_op jit(solution)/shard_map/columns_of/pallas_call | solution.py:56
  167.3 37.3 %collective-permute-done.25.refs_4_ = f32[1,1024]{1,0:T(1,128)S(1)} collective-permute-done((f32[1,1024]{1,0:T(1,128)S(1)}, f32[1,1024]{1,0:T(1,128)S(1)}, u32[]{:S(2)}, u32[]{:S(2)}) %collective-permute-start.25) | collective-permute-done | bytes 4128 | tf_op jit(solution)/shard_map/ppermute | solution.py:392
  206.8 2.8 final_scales.1
  214.8 17.2 %gradients.4 = (bf16[128,2048]{1,0:T(8,128)(2,1)}, bf16[128,2048]{1,0:T(8,128)(2,1)}, bf16[128,2048]{1,0:T(8,128)(2,1)}, bf16[128,2048]{1,0:T(8,128)(2,1)}, f32[1024,512]{1,0:T(8,128)}) custom-call(s32[8]{0:T(128)} %stack.32.places, bf16[1024,512]{1,0:T(8,128)(2,1)} %get-tuple-element.81.teacher_embed, bf16[1024,512]{1,0:T(8,128)(2,1)} %copy-done, ...), custom_call_target="tpu_custom_call" | custom-call | flops 8589934592 | bytes 10485760 | tf_op jit(solution)/shard_map/gradients/pallas_call | solution.py:311
  232.0 19.8 %gradients.5 = (bf16[128,2560]{1,0:T(8,128)(2,1)}, bf16[128,2560]{1,0:T(8,128)(2,1)}, bf16[128,2560]{1,0:T(8,128)(2,1)}, bf16[128,2560]{1,0:T(8,128)(2,1)}, f32[1024,512]{1,0:T(8,128)}) custom-call(s32[8]{0:T(128)} %stack.32.places, bf16[1024,512]{1,0:T(8,128)(2,1)} %get-tuple-element.81.teacher_embed, bf16[1024,512]{1,0:T(8,128)(2,1)} %copy-done, ...), custom_call_target="tpu_custom_call" | custom-call | flops 10737418240 | bytes 12058624 | tf_op jit(solution)/shard_map/gradients/pallas_call | solution.py:311
  253.5 17.2 %gradients.6 = (bf16[128,2048]{1,0:T(8,128)(2,1)}, bf16[128,2048]{1,0:T(8,128)(2,1)}, bf16[128,2048]{1,0:T(8,128)(2,1)}, bf16[128,2048]{1,0:T(8,128)(2,1)}, f32[1024,512]{1,0:T(8,128)}) custom-call(s32[8]{0:T(128)} %stack.32.places, bf16[1024,512]{1,0:T(8,128)(2,1)} %get-tuple-element.81.teacher_embed, bf16[1024,512]{1,0:T(8,128)(2,1)} %copy-done, ...), custom_call_target="tpu_custom_call" | custom-call | flops 8589934592 | bytes 10485760 | tf_op jit(solution)/shard_map/gradients/pallas_call | solution.py:311
  270.6 14.8 %collective-permute-done.18.arrived = bf16[512,1536]{1,0:T(8,128)(2,1)} collective-permute-done((bf16[512,1536]{1,0:T(8,128)(2,1)}, bf16[512,1536]{1,0:T(8,128)(2,1)}, u32[]{:S(2)}, u32[]{:S(2)}) %collective-permute-start.18) | collective-permute-done | bytes 1572896 | tf_op jit(solution)/shard_map/ppermute | solution.py:392
  285.5 14.1 %gradients.7 = (bf16[128,1536]{1,0:T(8,128)(2,1)}, bf16[128,1536]{1,0:T(8,128)(2,1)}, bf16[128,1536]{1,0:T(8,128)(2,1)}, bf16[128,1536]{1,0:T(8,128)(2,1)}, f32[1024,512]{1,0:T(8,128)}) custom-call(s32[8]{0:T(128)} %stack.32.places, bf16[1024,512]{1,0:T(8,128)(2,1)} %get-tuple-element.81.teacher_embed, bf16[1024,512]{1,0:T(8,128)(2,1)} %copy-done, ...), custom_call_target="tpu_custom_call" | custom-call | flops 6442450944 | bytes 8912896 | tf_op jit(solution)/shard_map/gradients/pallas_call | solution.py:311
  301.1 2.8 collective-permute-done.42
  308.3 11.2 %collective-permute-done.43 = f32[256,512]{1,0:T(8,128)S(1)} collective-permute-done((f32[256,512]{1,0:T(8,128)S(1)}, f32[256,512]{1,0:T(8,128)S(1)}, u32[]{:S(2)}, u32[]{:S(2)}) %collective-permute-start.43) | collective-permute-done | bytes 524320 | tf_op jit(solution)/shard_map/ppermute | solution.py:423
  324.5 7.4 %collective-permute-done.41.refs_3_ = bf16[128,2048]{1,0:T(8,128)(2,1)S(1)} collective-permute-done((bf16[128,2048]{1,0:T(8,128)(2,1)}, bf16[128,2048]{1,0:T(8,128)(2,1)S(1)}, u32[]{:S(2)}, u32[]{:S(2)}) %collective-permute-start.41) | collective-permute-done | bytes 524320 | tf_op jit(solution)/shard_map/ppermute | solution.py:391
  337.9 20.1 %collective-permute-done.34.refs_2_ = bf16[128,2048]{1,0:T(8,128)(2,1)S(1)} collective-permute-done((bf16[128,2048]{1,0:T(8,128)(2,1)}, bf16[128,2048]{1,0:T(8,128)(2,1)S(1)}, u32[]{:S(2)}, u32[]{:S(2)}) %collective-permute-start.34) | collective-permute-done | bytes 524320 | tf_op jit(solution)/shard_map/ppermute | solution.py:392
  361.3 9.8 %collective-permute-done.38.refs_3_ = bf16[128,2560]{1,0:T(8,128)(2,1)S(1)} collective-permute-done((bf16[128,2560]{1,0:T(8,128)(2,1)}, bf16[128,2560]{1,0:T(8,128)(2,1)S(1)}, u32[]{:S(2)}, u32[]{:S(2)}) %collective-permute-start.38) | collective-permute-done | bytes 655392 | tf_op jit(solution)/shard_map/ppermute | solution.py:391
  372.6 4.1 %placed_pieces.4.refs_4_ = bf16[128,32768]{1,0:T(8,128)(2,1)} custom-call(s32[8]{0:T(128)} %stack.32.places, bf16[128,2048]{1,0:T(8,128)(2,1)} %get-tuple-element.75.refs_0_, bf16[128,2048]{1,0:T(8,128)(2,1)} %copy-done.8, bf16[128,2048]{1,0:T(8,128)(2,1)} %copy-done.9, bf16[128,2048]{1,0:T(8,128)(2,1)} %copy-done.10), custom_call_target="tpu_custom_call" | custom-call | bytes 4194304 | tf_op jit(solution)/shard_map/placed_pieces/pallas_call | solution.py:371
  376.7 9.1 %placed_pieces.5.refs_4_ = bf16[128,32768]{1,0:T(8,128)(2,1)} custom-call(s32[8]{0:T(128)} %stack.32.places, bf16[128,2560]{1,0:T(8,128)(2,1)} %get-tuple-element.71.refs_0_, bf16[128,2560]{1,0:T(8,128)(2,1)} %copy-done.3, bf16[128,2560]{1,0:T(8,128)(2,1)} %copy-done.4, bf16[128,2560]{1,0:T(8,128)(2,1)} %copy-done.5, ...), custom_call_target="tpu_custom_call", output_to_operand_aliasing={{}: (5, {})} | custom-call | bytes 5242880 | tf_op jit(solution)/shard_map/placed_pieces/pallas_call | solution.py:371
  385.8 4.1 %placed_pieces.6.refs_4_ = bf16[128,32768]{1,0:T(8,128)(2,1)} custom-call(s32[8]{0:T(128)} %stack.32.places, bf16[128,2048]{1,0:T(8,128)(2,1)} %get-tuple-element.67.refs_0_, bf16[128,2048]{1,0:T(8,128)(2,1)} %copy-done.6, bf16[128,2048]{1,0:T(8,128)(2,1)} %copy-done.7, ...), custom_call_target="tpu_custom_call", output_to_operand_aliasing={{}: (5, {})} | custom-call | bytes 4194304 | tf_op jit(solution)/shard_map/placed_pieces/pallas_call | solution.py:371
  389.9 1.8 collective-permute-done.31.refs_2_
  391.8 7.5 %collective-permute-done.32.refs_3_ = bf16[128,1536]{1,0:T(8,128)(2,1)} collective-permute-done((bf16[128,1536]{1,0:T(8,128)(2,1)}, bf16[128,1536]{1,0:T(8,128)(2,1)}, u32[]{:S(2)}, u32[]{:S(2)}) %collective-permute-start.32) | collective-permute-done | bytes 393248 | tf_op jit(solution)/shard_map/ppermute | solution.py:391
  399.3 6.1 %placed_pieces.7 = bf16[128,32768]{1,0:T(8,128)(2,1)} custom-call(s32[8]{0:T(128)} %stack.32.places, bf16[128,1536]{1,0:T(8,128)(2,1)} %get-tuple-element.63.refs_0_, bf16[128,1536]{1,0:T(8,128)(2,1)} %collective-permute-done.30.refs_1_, bf16[128,1536]{1,0:T(8,128)(2,1)} %collective-permute-done.31.refs_2_, ...), custom_call_target="tpu_custom_call", output_to_operand_aliasing={{}: (5, {})} | custom-call | bytes 3145728 | tf_op jit(solution)/shard_map/placed_pieces/pallas_call | solution.py:371
  (163 shorter events, 62.0 us)
Async XLA Ops:
  0.6 8.4 %collective-permute-start.2 = (bf16[512,512]{1,0:T(8,128)(2,1)}, bf16[512,512]{1,0:T(8,128)(2,1)S(1)}, u32[]{:S(2)}, u32[]{:S(2)}) collective-permute-start(bf16[512,512]{1,0:T(8,128)(2,1)} %bitcast.71), channel_id=1, source_target_pairs={{0,1},{1,0},{2,3},{3,2},{4,5},{5,4},{6,7},{7,6},{8,9},{9,8},{10,11... | collective-permute-start | bytes 1572872 | tf_op jit(solution)/shard_map/ppermute | solution.py:392
  2.0 5.3 %collective-permute-start = (bf16[64,512]{1,0:T(8,128)(2,1)S(1)}, bf16[64,512]{1,0:T(8,128)(2,1)S(1)}, u32[]{:S(2)}, u32[]{:S(2)}) collective-permute-start(bf16[64,512]{1,0:T(8,128)(2,1)S(1)} %dynamic-slice_bitcast_fusion.6), channel_id=1, source_target_pairs={{0,16},{16,0},{1,17},{17,1},{2,18},{18,2},{3,19},{19,3},{4,20},{20... | collective-permute-start | bytes 196616 | tf_op jit(solution)/shard_map/ppermute | solution.py:392
  7.3 43.2 %collective-permute-start.1 = (bf16[64,512]{1,0:T(8,128)(2,1)S(1)}, bf16[64,512]{1,0:T(8,128)(2,1)S(1)}, u32[]{:S(2)}, u32[]{:S(2)}) collective-permute-start(bf16[64,512]{1,0:T(8,128)(2,1)S(1)} %collective-permute-done), channel_id=1, source_target_pairs={{0,2},{2,0},{4,6},{6,4},{8,10},{10,8},{12,14},{14,12},{1,3},{3,1},... | collective-permute-start | bytes 196616 | tf_op jit(solution)/shard_map/ppermute | solution.py:423
  53.2 5.5 %collective-permute-start.9 = (f32[1,1024]{1,0:T(1,128)S(1)}, f32[1,1024]{1,0:T(1,128)S(1)}, u32[]{:S(2)}, u32[]{:S(2)}) collective-permute-start(f32[1,1024]{1,0:T(1,128)S(1)} %add_add_fusion.2.refs_0_), channel_id=1, source_target_pairs={{0,12},{1,13},{2,14},{3,15},{4,8},{5,9},{6,10},{7,11},{8,4},{9,5},... | collective-permute-start | bytes 12296 | tf_op jit(solution)/shard_map/ppermute | solution.py:408
  99.8 6.4 %collective-permute-start.3 = (bf16[128,512]{1,0:T(8,128)(2,1)S(1)}, bf16[128,512]{1,0:T(8,128)(2,1)S(1)}, u32[]{:S(2)}, u32[]{:S(2)}) collective-permute-start(bf16[128,512]{1,0:T(8,128)(2,1)S(1)} %pad_maximum_fusion.5), channel_id=1, source_target_pairs={{0,4},{2,6},{4,0},{6,2},{8,12},{10,14},{12,8},{14,10},{1,5},{3,7},... | collective-permute-start | bytes 393224 | tf_op jit(solution)/shard_map/ppermute | solution.py:423
  99.9 113.3 %collective-permute-start.29 = (bf16[512,2048]{1,0:T(8,128)(2,1)}, bf16[512,2048]{1,0:T(8,128)(2,1)}, u32[]{:S(2)}, u32[]{:S(2)}) collective-permute-start(bf16[512,2048]{1,0:T(8,128)(2,1)} %get-tuple-element.59), channel_id=1, source_target_pairs={{0,16},{16,0},{1,17},{17,1},{2,18},{18,2},{3,19},{19,3},{4,20},{20... | collective-permute-start | bytes 6291464 | tf_op jit(solution)/shard_map/ppermute | solution.py:392
  101.5 130.5 %collective-permute-start.28 = (bf16[512,2560]{1,0:T(8,128)(2,1)}, bf16[512,2560]{1,0:T(8,128)(2,1)}, u32[]{:S(2)}, u32[]{:S(2)}) collective-permute-start(bf16[512,2560]{1,0:T(8,128)(2,1)} %get-tuple-element.58), channel_id=1, source_target_pairs={{0,16},{16,0},{1,17},{17,1},{2,18},{18,2},{3,19},{19,3},{4,20},{20... | collective-permute-start | bytes 7864328 | tf_op jit(solution)/shard_map/ppermute | solution.py:392
  103.4 5.5 %collective-permute-start.16 = (f32[1,1024]{1,0:T(1,128)S(1)}, f32[1,1024]{1,0:T(1,128)S(1)}, u32[]{:S(2)}, u32[]{:S(2)}) collective-permute-start(f32[1,1024]{1,0:T(1,128)S(1)} %add_add_fusion.1.refs_0_), channel_id=1, source_target_pairs={{0,12},{1,13},{2,14},{3,15},{4,8},{5,9},{6,10},{7,11},{8,4},{9,5},... | collective-permute-start | bytes 12296 | tf_op jit(solution)/shard_map/ppermute | solution.py:408
  105.6 5.0 %collective-permute-start.15 = (f32[1,1024]{1,0:T(1,128)S(1)}, f32[1,1024]{1,0:T(1,128)S(1)}, u32[]{:S(2)}, u32[]{:S(2)}) collective-permute-start(f32[1,1024]{1,0:T(1,128)S(1)} %add_add_fusion.1.refs_0_), channel_id=1, source_target_pairs={{0,8},{1,9},{2,10},{3,11},{4,12},{5,13},{6,14},{7,15},{8,0},{9,1},... | collective-permute-start | bytes 12296 | tf_op jit(solution)/shard_map/ppermute | solution.py:408
  108.9 38.2 %collective-permute-start.10 = (bf16[256,512]{1,0:T(8,128)(2,1)S(1)}, bf16[256,512]{1,0:T(8,128)(2,1)S(1)}, u32[]{:S(2)}, u32[]{:S(2)}) collective-permute-start(bf16[256,512]{1,0:T(8,128)(2,1)S(1)} %pad_maximum_fusion.4), channel_id=1, source_target_pairs={{0,8},{2,10},{4,12},{6,14},{8,0},{10,2},{12,4},{14,6},{1,9},{3,11}... | collective-permute-start | bytes 786440 | tf_op jit(solution)/shard_map/ppermute | solution.py:423
  147.2 62.5 %collective-permute-start.17 = (bf16[512,512]{1,0:T(8,128)(2,1)S(1)}, bf16[512,512]{1,0:T(8,128)(2,1)S(1)}, u32[]{:S(2)}, u32[]{:S(2)}) collective-permute-start(bf16[512,512]{1,0:T(8,128)(2,1)S(1)} %pad_maximum_fusion.3), channel_id=1, source_target_pairs={{0,1},{1,0},{2,3},{3,2},{4,5},{5,4},{6,7},{7,6},{8,9},{9,8},{10,11... | collective-permute-start | bytes 1572872 | tf_op jit(solution)/shard_map/ppermute | solution.py:392
  152.0 5.5 %collective-permute-start.24 = (f32[1,1024]{1,0:T(1,128)S(1)}, f32[1,1024]{1,0:T(1,128)S(1)}, u32[]{:S(2)}, u32[]{:S(2)}) collective-permute-start(f32[1,1024]{1,0:T(1,128)S(1)} %add_add_fusion.refs_0_), channel_id=1, source_target_pairs={{0,12},{1,13},{2,14},{3,15},{4,8},{5,9},{6,10},{7,11},{8,4},{9,5},... | collective-permute-start | bytes 12296 | tf_op jit(solution)/shard_map/ppermute | solution.py:408
  158.3 47.9 %collective-permute-start.26 = (f32[1,8192]{1,0:T(1,128)S(1)}, f32[1,8192]{1,0:T(1,128)S(1)}, u32[]{:S(2)}, u32[]{:S(2)}) collective-permute-start(f32[1,8192]{1,0:T(1,128)S(1)} %copy-done.21), channel_id=1, source_target_pairs={{0,16},{16,0},{1,17},{17,1},{2,18},{18,2},{3,19},{19,3},{4,20},{20... | collective-permute-start | bytes 98312 | tf_op jit(solution)/shard_map/ppermute | solution.py:392
  161.1 43.5 %collective-permute-start.25 = (f32[1,1024]{1,0:T(1,128)S(1)}, f32[1,1024]{1,0:T(1,128)S(1)}, u32[]{:S(2)}, u32[]{:S(2)}) collective-permute-start(f32[1,1024]{1,0:T(1,128)S(1)} %add_divide_fusion), channel_id=1, source_target_pairs={{0,16},{16,0},{1,17},{17,1},{2,18},{18,2},{3,19},{19,3},{4,20},{20... | collective-permute-start | bytes 12296 | tf_op jit(solution)/shard_map/ppermute | solution.py:392
  204.7 48.8 %collective-permute-start.27 = (bf16[512,2048]{1,0:T(8,128)(2,1)}, bf16[512,2048]{1,0:T(8,128)(2,1)}, u32[]{:S(2)}, u32[]{:S(2)}) collective-permute-start(bf16[512,2048]{1,0:T(8,128)(2,1)} %columns_of.1), channel_id=1, source_target_pairs={{0,16},{16,0},{1,17},{17,1},{2,18},{18,2},{3,19},{19,3},{4,20},{20... | collective-permute-start | bytes 6291464 | tf_op jit(solution)/shard_map/ppermute | solution.py:392
  206.2 79.3 %collective-permute-start.18 = (bf16[512,1536]{1,0:T(8,128)(2,1)}, bf16[512,1536]{1,0:T(8,128)(2,1)}, u32[]{:S(2)}, u32[]{:S(2)}) collective-permute-start(bf16[512,1536]{1,0:T(8,128)(2,1)} %get-tuple-element.52), channel_id=1, source_target_pairs={{0,16},{16,0},{1,17},{17,1},{2,18},{18,2},{3,19},{19,3},{4,20},{20... | collective-permute-start | bytes 4718600 | tf_op jit(solution)/shard_map/ppermute | solution.py:392
  305.4 14.0 %collective-permute-start.43 = (f32[256,512]{1,0:T(8,128)S(1)}, f32[256,512]{1,0:T(8,128)S(1)}, u32[]{:S(2)}, u32[]{:S(2)}) collective-permute-start(f32[256,512]{1,0:T(8,128)S(1)} %bitcast.72), channel_id=1, source_target_pairs={{0,2},{2,0},{4,6},{6,4},{8,10},{10,8},{12,14},{14,12},{1,3},{3,1},... | collective-permute-start | bytes 1572872 | tf_op jit(solution)/shard_map/ppermute | solution.py:423
  306.4 14.7 %collective-permute-start.39 = (bf16[128,2048]{1,0:T(8,128)(2,1)}, bf16[128,2048]{1,0:T(8,128)(2,1)S(1)}, u32[]{:S(2)}, u32[]{:S(2)}) collective-permute-start(bf16[128,2048]{1,0:T(8,128)(2,1)} %get-tuple-element.76), channel_id=1, source_target_pairs={{0,1},{1,0},{2,3},{3,2},{4,5},{5,4},{6,7},{7,6},{8,9},{9,8},{10,11... | collective-permute-start | bytes 1572872 | tf_op jit(solution)/shard_map/ppermute | solution.py:392
  306.4 17.0 %collective-permute-start.40 = (bf16[128,2048]{1,0:T(8,128)(2,1)}, bf16[128,2048]{1,0:T(8,128)(2,1)S(1)}, u32[]{:S(2)}, u32[]{:S(2)}) collective-permute-start(bf16[128,2048]{1,0:T(8,128)(2,1)} %get-tuple-element.77), channel_id=1, source_target_pairs={{0,16},{16,0},{1,17},{17,1},{2,18},{18,2},{3,19},{19,3},{4,20},{20... | collective-permute-start | bytes 1572872 | tf_op jit(solution)/shard_map/ppermute | solution.py:392
  308.0 23.9 %collective-permute-start.41 = (bf16[128,2048]{1,0:T(8,128)(2,1)}, bf16[128,2048]{1,0:T(8,128)(2,1)S(1)}, u32[]{:S(2)}, u32[]{:S(2)}) collective-permute-start(bf16[128,2048]{1,0:T(8,128)(2,1)} %get-tuple-element.78), channel_id=1, source_target_pairs={{0,17},{1,16},{16,1},{17,0},{2,19},{3,18},{18,3},{19,2},{4,21},{5,... | collective-permute-start | bytes 1572872 | tf_op jit(solution)/shard_map/ppermute | solution.py:391
  319.6 14.5 %collective-permute-start.44 = (f32[128,512]{1,0:T(8,128)S(1)}, f32[128,512]{1,0:T(8,128)S(1)}, u32[]{:S(2)}, u32[]{:S(2)}) collective-permute-start(f32[128,512]{1,0:T(8,128)S(1)} %bitcast.73), channel_id=1, source_target_pairs={{0,4},{2,6},{4,0},{6,2},{8,12},{10,14},{12,8},{14,10},{1,5},{3,7},... | collective-permute-start | bytes 786440 | tf_op jit(solution)/shard_map/ppermute | solution.py:423
  321.1 37.2 %collective-permute-start.36 = (bf16[128,2560]{1,0:T(8,128)(2,1)}, bf16[128,2560]{1,0:T(8,128)(2,1)S(1)}, u32[]{:S(2)}, u32[]{:S(2)}) collective-permute-start(bf16[128,2560]{1,0:T(8,128)(2,1)} %get-tuple-element.72), channel_id=1, source_target_pairs={{0,1},{1,0},{2,3},{3,2},{4,5},{5,4},{6,7},{7,6},{8,9},{9,8},{10,11... | collective-permute-start | bytes 1966088 | tf_op jit(solution)/shard_map/ppermute | solution.py:392
  321.9 37.7 %collective-permute-start.37 = (bf16[128,2560]{1,0:T(8,128)(2,1)}, bf16[128,2560]{1,0:T(8,128)(2,1)S(1)}, u32[]{:S(2)}, u32[]{:S(2)}) collective-permute-start(bf16[128,2560]{1,0:T(8,128)(2,1)} %get-tuple-element.73), channel_id=1, source_target_pairs={{0,16},{16,0},{1,17},{17,1},{2,18},{18,2},{3,19},{19,3},{4,20},{20... | collective-permute-start | bytes 1966088 | tf_op jit(solution)/shard_map/ppermute | solution.py:392
  324.2 12.1 %collective-permute-start.33 = (bf16[128,2048]{1,0:T(8,128)(2,1)}, bf16[128,2048]{1,0:T(8,128)(2,1)S(1)}, u32[]{:S(2)}, u32[]{:S(2)}) collective-permute-start(bf16[128,2048]{1,0:T(8,128)(2,1)} %get-tuple-element.68), channel_id=1, source_target_pairs={{0,1},{1,0},{2,3},{3,2},{4,5},{5,4},{6,7},{7,6},{8,9},{9,8},{10,11... | collective-permute-start | bytes 1572872 | tf_op jit(solution)/shard_map/ppermute | solution.py:392
  332.6 25.3 %collective-permute-start.34 = (bf16[128,2048]{1,0:T(8,128)(2,1)}, bf16[128,2048]{1,0:T(8,128)(2,1)S(1)}, u32[]{:S(2)}, u32[]{:S(2)}) collective-permute-start(bf16[128,2048]{1,0:T(8,128)(2,1)} %get-tuple-element.69), channel_id=1, source_target_pairs={{0,16},{16,0},{1,17},{17,1},{2,18},{18,2},{3,19},{19,3},{4,20},{20... | collective-permute-start | bytes 1572872 | tf_op jit(solution)/shard_map/ppermute | solution.py:392
  334.8 36.4 %collective-permute-start.38 = (bf16[128,2560]{1,0:T(8,128)(2,1)}, bf16[128,2560]{1,0:T(8,128)(2,1)S(1)}, u32[]{:S(2)}, u32[]{:S(2)}) collective-permute-start(bf16[128,2560]{1,0:T(8,128)(2,1)} %get-tuple-element.74), channel_id=1, source_target_pairs={{0,17},{1,16},{16,1},{17,0},{2,19},{3,18},{18,3},{19,2},{4,21},{5,... | collective-permute-start | bytes 1966088 | tf_op jit(solution)/shard_map/ppermute | solution.py:391
  336.4 23.7 %collective-permute-start.45 = (f32[64,512]{1,0:T(8,128)S(1)}, f32[64,512]{1,0:T(8,128)S(1)}, u32[]{:S(2)}, u32[]{:S(2)}) collective-permute-start(f32[64,512]{1,0:T(8,128)S(1)} %dynamic-slice_bitcast_fusion.5), channel_id=1, source_target_pairs={{0,8},{2,10},{4,12},{6,14},{8,0},{10,2},{12,4},{14,6},{1,9},{3,11}... | collective-permute-start | bytes 393224 | tf_op jit(solution)/shard_map/ppermute | solution.py:423
  358.0 27.9 %collective-permute-start.35 = (bf16[128,2048]{1,0:T(8,128)(2,1)}, bf16[128,2048]{1,0:T(8,128)(2,1)}, u32[]{:S(2)}, u32[]{:S(2)}) collective-permute-start(bf16[128,2048]{1,0:T(8,128)(2,1)} %get-tuple-element.70), channel_id=1, source_target_pairs={{0,17},{1,16},{16,1},{17,0},{2,19},{3,18},{18,3},{19,2},{4,21},{5,... | collective-permute-start | bytes 1572872 | tf_op jit(solution)/shard_map/ppermute | solution.py:391
  358.3 31.6 %collective-permute-start.30 = (bf16[128,1536]{1,0:T(8,128)(2,1)}, bf16[128,1536]{1,0:T(8,128)(2,1)}, u32[]{:S(2)}, u32[]{:S(2)}) collective-permute-start(bf16[128,1536]{1,0:T(8,128)(2,1)} %get-tuple-element.64), channel_id=1, source_target_pairs={{0,1},{1,0},{2,3},{3,2},{4,5},{5,4},{6,7},{7,6},{8,9},{9,8},{10,11... | collective-permute-start | bytes 1179656 | tf_op jit(solution)/shard_map/ppermute | solution.py:392
  359.6 32.1 %collective-permute-start.31 = (bf16[128,1536]{1,0:T(8,128)(2,1)}, bf16[128,1536]{1,0:T(8,128)(2,1)}, u32[]{:S(2)}, u32[]{:S(2)}) collective-permute-start(bf16[128,1536]{1,0:T(8,128)(2,1)} %get-tuple-element.65), channel_id=1, source_target_pairs={{0,16},{16,0},{1,17},{17,1},{2,18},{18,2},{3,19},{19,3},{4,20},{20... | collective-permute-start | bytes 1179656 | tf_op jit(solution)/shard_map/ppermute | solution.py:392
  360.1 39.2 %collective-permute-start.32 = (bf16[128,1536]{1,0:T(8,128)(2,1)}, bf16[128,1536]{1,0:T(8,128)(2,1)}, u32[]{:S(2)}, u32[]{:S(2)}) collective-permute-start(bf16[128,1536]{1,0:T(8,128)(2,1)} %get-tuple-element.66), channel_id=1, source_target_pairs={{0,17},{1,16},{16,1},{17,0},{2,19},{3,18},{18,3},{19,2},{4,21},{5,... | collective-permute-start | bytes 1179656 | tf_op jit(solution)/shard_map/ppermute | solution.py:391
  371.2 34.2 %collective-permute-start.46 = (f32[64,256]{1,0:T(8,128)S(1)}, f32[64,256]{1,0:T(8,128)S(1)}, u32[]{:S(2)}, u32[]{:S(2)}) collective-permute-start(f32[64,256]{1,0:T(8,128)S(1)} %bitcast.74), channel_id=1, source_target_pairs={{0,16},{16,0},{1,17},{17,1},{2,18},{18,2},{3,19},{19,3},{4,20},{20... | collective-permute-start | bytes 196616 | tf_op jit(solution)/shard_map/ppermute | solution.py:392
  (43 other events, 282.3 us)
where the time goes:
time: 409 us; the launch traced here: 406 us
  Pallas kernels  207 us (51%)
  waiting for transfers between devices  133 us (33%)
  starting transfers between devices  43.8 us (11%)
  local copies, waits for them, and re-layouts  12 us (3%)
  other arithmetic  9.44 us (2%)
    pallas_call x3, Pallas kernels, sinkhorn_pass(): pl.pallas_call(functools.partial(pass_body, first, len(parts), tiles), ou...  108 us
    ppermute x18, waiting for transfers between devices, swapped(): return lax.ppermute(value, axes[0], [(0, 1), (1, 0)])  77.9 us
    pallas_call x4, Pallas kernels, gradients(): pl.pallas_call(grads_body, out_shape=(piece,) * 4 + (jax.ShapeDtypeStruct...  68.2 us
    ppermute x4, waiting for transfers between devices, swapped(): return lax.ppermute(value, axes, [(0, 3), (1, 2), (2, 1), (3, 0)])  24.7 us
    pallas_call x4, Pallas kernels, placed_pieces(): pl.pallas_call(place_body, out_shape=jax.ShapeDtypeStruct((rows, block_wi...  23.4 us
    ppermute x18, starting transfers between devices, swapped(): return lax.ppermute(value, axes[0], [(0, 1), (1, 0)])  18.5 us
    ppermute x18, starting transfers between devices, summands(): parts.append(lax.ppermute(parts[0], axes, pairs))  17.3 us
    ppermute x18, waiting for transfers between devices, summands(): parts.append(lax.ppermute(parts[0], axes, pairs))  16.2 us
  transfers between devices with their start and end apart: 47, of which 23 were waited for; matrix products, arithmetic and copies ran while one was open for 3% of the time, Pallas kernels for 39%

commit v1 on v0

v1 whole, which is shorter than its diff:
```python
import functools

import jax
import jax.numpy as jnp
from jax import lax
from jax.experimental import pallas as pl
from jax.experimental.pallas import tpu as pltpu
from jax.sharding import PartitionSpec as P


ITERS = 3
LOG2E = 1.4426950408889634
SHARES = (1, 5, 2, 4, 4)
CHUNKS = len(SHARES)
SLICED = 2
GRAD_ORDER = (2, 1, 3, 4, 0)
ROWS = 256
LINES = 16
NT = (((1,), (1,)), ((), ()))


def whole(shape):
    return pl.BlockSpec(shape, lambda *_: (0,) * len(shape), pipeline_mode=pl.Buffered(1))


def cost(flops, bytes_accessed, transcendentals):
    return pl.CostEstimate(
        flops=flops, bytes_accessed=bytes_accessed, transcendentals=transcendentals
    )


def tile_width(quarter_width):
    return 512 if quarter_width % 8192 == 0 else 128


def chunk_tiles(quarter_width):
    tiles = quarter_width // tile_width(quarter_width)
    if tiles % sum(SHARES) == 0:
        counts = [tiles * share // sum(SHARES) for share in SHARES]
    else:
        pairs, rest = divmod(tiles // 2 - 1, CHUNKS - SLICED)
        counts = [1] * SLICED + [2 * (pairs + (n < rest)) for n in range(CHUNKS - SLICED)]
    return [(sum(counts[:n]), count) for n, count in enumerate(counts)]


def pass_tiles(quarter_width):
    tile = 2 * tile_width(quarter_width)
    return tile, quarter_width // tile


def pass_chunks(quarter_width):
    return [(begin // 2, count // 2) for begin, count in chunk_tiles(quarter_width)[SLICED:]]


def lane_tiles(value, width):
    return jnp.concatenate([value] * (width // value.shape[1]), axis=1)


def columns_body(tile, begin, places, matrix, target, arrived):
    width = target.shape[1]
    start = pl.multiple_of(places[2] * (matrix.shape[1] // 4) + begin * tile, tile)
    copy = pltpu.make_async_copy(matrix.at[:, pl.ds(start, width)], target, arrived)
    copy.start()
    copy.wait()


def columns_of(places, matrix, chunk):
    depth = matrix.shape[0]
    quarter_width = matrix.shape[1] // 4
    tile = tile_width(quarter_width)
    begin, count = chunk_tiles(quarter_width)[chunk]
    width = count * tile
    return pl.pallas_call(
        functools.partial(columns_body, tile, begin),
        out_shape=jax.ShapeDtypeStruct((depth, width), matrix.dtype),
        grid_spec=pltpu.PrefetchScalarGridSpec(
            num_scalar_prefetch=1,
            grid=(1,),
            in_specs=[pl.BlockSpec(memory_space=pl.ANY)],
            out_specs=pl.BlockSpec(memory_space=pltpu.VMEM),
            scratch_shapes=[pltpu.SemaphoreType.DMA],
        ),
        cost_estimate=cost(0, 4 * depth * width, 0),
        name="columns_of",
    )(places, matrix)


def reciprocal_rows(parts, crops):
    total = parts[0][...]
    for part in parts[1:]:
        total = total + part[...]
    return jnp.transpose(jnp.broadcast_to(1.0 / total, (128, crops)))


def folded(value):
    total = value[:, :128]
    for lane in range(128, value.shape[1], 128):
        total += value[:, lane : lane + 128]
    return total


def finish_tile(places, tiles, step, total, powers, own_factor, partner_factor, sums):
    factor = jnp.where(
        places[0] == 1, 1.0, 1.0 / jnp.sum(total, axis=0, keepdims=True)
    )
    owned = step // tiles == places[0]

    @pl.when(owned)
    def _():
        own_factor[...] = factor

    @pl.when(jnp.logical_not(owned))
    def _():
        partner_factor[...] = factor

    for start in range(0, powers.shape[0], LINES):
        rows = pl.ds(start, LINES)
        sums[rows, :] += folded(powers[rows, :] * factor)


def finish_pass(row_sums, sums):
    @pl.when(pl.program_id(0) == pl.num_programs(0) - 1)
    def _():
        row_sums[...] = lax.dot_general(
            jnp.ones((8, 128), jnp.float32),
            sums[...],
            NT,
            precision=lax.Precision.HIGHEST,
            preferred_element_type=jnp.float32,
        )[:1]


def first_body(tiles, places, scale, embed, weight, *refs):
    row_sums, own_factor, partner_factor, powers = refs[:4]
    sent, sums = refs[4:-1], refs[-1]
    step = pl.program_id(0)
    crops = embed.shape[0]
    width = weight.shape[1]

    @pl.when(step == 0)
    def _():
        sums[...] = jnp.zeros_like(sums)

    block = weight[...]
    total = jnp.zeros((8, width), jnp.float32)
    for start in range(0, crops, ROWS):
        rows = pl.ds(start, ROWS)
        scores = jnp.dot(embed[rows, :], block, preferred_element_type=jnp.float32)
        part = jnp.exp2(scores * scale[0])
        powers[rows, :] = part
        total += jnp.sum(part.reshape(ROWS // 8, 8, width), axis=0)
    foreign = step // tiles != places[0]
    here = lax.rem(step, tiles)
    for (begin, count), piece in zip(pass_chunks(tiles * width), sent):

        @pl.when(foreign & (here >= begin) & (here < begin + count))
        def _(piece=piece):
            piece[...] = block

    finish_tile(places, tiles, step, total, powers, own_factor, partner_factor, sums)
    finish_pass(row_sums, sums)


def later_body(nparts, tiles, places, powers, *refs):
    parts, refs = refs[:nparts], refs[nparts:]
    row_sums, own_factor, partner_factor, sums, row_scale = refs
    group, crops, width = powers.shape

    @pl.when(pl.program_id(0) == 0)
    def _():
        sums[...] = jnp.zeros_like(sums)
        row_scale[...] = reciprocal_rows(parts, crops)

    for place in range(group):
        tile = powers.at[place]
        lanes = pl.ds(place * width, width)
        total = jnp.zeros((8, width), jnp.float32)
        for start in range(0, crops, 8):
            rows = pl.ds(start, 8)
            total += tile[rows, :] * lane_tiles(row_scale[rows, :], width)
        finish_tile(
            places,
            tiles,
            pl.program_id(0) * group,
            total,
            tile,
            own_factor.at[:, lanes],
            partner_factor.at[:, lanes],
            sums,
        )
    finish_pass(row_sums, sums)


def pass_outputs(crops, quarter_width, group=1):
    tile, tiles = pass_tiles(quarter_width)
    tile, tiles = tile * group, tiles // group

    def owner_spec(partner):
        def index(t, places):
            begin = tiles * (1 - places[0] if partner else places[0])
            return (0, jnp.clip(t - begin, 0, tiles - 1))

        return pl.BlockSpec((1, tile), index)

    factor_shape = jax.ShapeDtypeStruct((1, quarter_width), jnp.float32)
    shapes = [jax.ShapeDtypeStruct((1, crops), jnp.float32), factor_shape, factor_shape]
    return shapes, [whole((1, crops)), owner_spec(False), owner_spec(True)]


def first_pass(places, scale, embed, weight):
    crops, depth = embed.shape
    quarter_width = weight.shape[1] // 4
    tile, tiles = pass_tiles(quarter_width)
    sent = pass_chunks(quarter_width)
    shapes, specs = pass_outputs(crops, quarter_width)

    def sent_spec(begin, count):
        def index(t, places):
            return (0, jnp.clip(t - tiles * (1 - places[0]) - begin, 0, count - 1))

        return pl.BlockSpec((depth, tile), index)

    return pl.pallas_call(
        functools.partial(first_body, tiles),
        out_shape=shapes
        + [jax.ShapeDtypeStruct((2 * tiles, crops, tile), jnp.float32)]
        + [jax.ShapeDtypeStruct((depth, count * tile), weight.dtype) for _, count in sent],
        grid_spec=pltpu.PrefetchScalarGridSpec(
            num_scalar_prefetch=1,
            grid=(2 * tiles,),
            in_specs=[
                pl.BlockSpec(memory_space=pltpu.SMEM),
                whole((crops, depth)),
                pl.BlockSpec((depth, tile), lambda t, places: (0, places[3] * 2 * tiles + t)),
            ],
            out_specs=specs
            + [pl.BlockSpec((None, crops, tile), lambda t, places: (t, 0, 0))]
            + [sent_spec(begin, count) for begin, count in sent],
            scratch_shapes=[pltpu.VMEM((crops, 128), jnp.float32)],
        ),
        cost_estimate=cost(
            4 * crops * depth * quarter_width,
            4 * depth * quarter_width + 8 * crops * quarter_width,
            2 * crops * quarter_width,
        ),
        name="first_pass",
    )(places, scale, embed, weight)


def later_pass(places, powers, parts):
    tiles, crops, tile = powers.shape[0] // 2, *powers.shape[1:]
    quarter_width = tiles * tile
    group = 2 if tiles % 2 == 0 else 1
    shapes, specs = pass_outputs(crops, quarter_width, group)
    return pl.pallas_call(
        functools.partial(later_body, len(parts), tiles),
        out_shape=shapes,
        grid_spec=pltpu.PrefetchScalarGridSpec(
            num_scalar_prefetch=1,
            grid=(2 * tiles // group,),
            in_specs=[
                pl.BlockSpec((group, crops, tile), lambda t, places: (t, 0, 0)),
                *[pl.BlockSpec(memory_space=pltpu.VMEM) for _ in parts],
            ],
            out_specs=specs,
            scratch_shapes=[
                pltpu.VMEM((crops, 128), jnp.float32),
                pltpu.VMEM((crops, 128), jnp.float32),
            ],
        ),
        cost_estimate=cost(8 * crops * quarter_width, 8 * crops * quarter_width, 0),
        name="later_pass",
    )(places, powers, *parts)


def scales_body(nparts, places, *refs):
    parts, (got_inverse, own_factor, got_factor) = refs[:nparts], refs[nparts : nparts + 3]
    row_scale, inverse_sum, column_scale = refs[-3:]
    crops = got_inverse.shape[1]
    mine = reciprocal_rows(parts, crops)
    theirs = jnp.transpose(jnp.broadcast_to(got_inverse[...], (128, crops)))
    teaches = places[0] == 0
    row_scale[...] = jnp.where(teaches, mine, theirs)
    inverse_sum[...] = jnp.where(teaches, theirs, mine)
    column_scale[...] = jnp.where(teaches, own_factor[...], got_factor[...])


def final_scales(places, parts, got_inverse, own_factor, got_factor, ahead):
    crops = got_inverse.shape[1]
    rows = jax.ShapeDtypeStruct((crops, 128), jnp.float32)
    return pl.pallas_call(
        functools.partial(scales_body, len(parts)),
        out_shape=[rows, rows, jax.ShapeDtypeStruct(own_factor.shape, jnp.float32)],
        grid_spec=pltpu.PrefetchScalarGridSpec(
            num_scalar_prefetch=1,
            grid=(1,),
            in_specs=[pl.BlockSpec(memory_space=pltpu.VMEM)] * (len(parts) + 3)
            + [pl.BlockSpec(memory_space=pl.ANY)] * len(ahead),
            out_specs=[pl.BlockSpec(memory_space=pltpu.VMEM)] * 2 + [whole(own_factor.shape)],
        ),
        cost_estimate=cost(0, 8 * crops * 128, 0),
        name="final_scales",
    )(places, *parts, got_inverse, own_factor, got_factor, *ahead)


def grads_body(first, places, other_embed, turned, own, arrived, powers, *refs):
    row_scale, inverse_sum, column_scale = refs[:3]
    embed_start = None if first else refs[3]
    pieces, embed_total, logit_grads = refs[-6:-2], refs[-2], refs[-1]
    crops, width = powers.shape
    quarter = turned.shape[0] // 4

    @pl.when(pl.program_id(0) == 0)
    def _():
        embed_total[...] = jnp.zeros_like(embed_total) if first else embed_start[...]

    def tile(student, divisor, teaches):
        block = arrived[...]
        student_block = student[...]
        factor = column_scale[...]
        for start in range(0, crops, ROWS):
            rows = pl.ds(start, ROWS)
            scores = jnp.dot(other_embed[rows, :], block, preferred_element_type=jnp.float32)
            computed = jnp.exp2(scores * (LOG2E / divisor))
            read = powers[rows, :]
            teacher, student_powers = (read, computed) if teaches else (computed, read)
            targets = (teacher * factor * lane_tiles(row_scale[rows, :], width)).astype(
                jnp.bfloat16
            )
            probs = student_powers * lane_tiles(inverse_sum[rows, :], width)
            grads = ((probs - targets.astype(jnp.float32)) * 10.0).astype(jnp.bfloat16)
            logit_grads[rows, :] = grads
            embed_total[rows, :] += lax.dot_general(
                grads, student_block, NT, preferred_element_type=jnp.float32
            )
        for place, piece in enumerate(pieces):
            piece[...] = jnp.dot(
                turned[pl.ds(place * quarter, quarter), :],
                logit_grads[...],
                preferred_element_type=jnp.float32,
            ).astype(piece.dtype)

    @pl.when(places[0] == 0)
    def _():
        tile(arrived, 0.1, True)

    @pl.when(places[0] == 1)
    def _():
        tile(own, 0.07, False)


def gradients(
    places, chunk, other_embed, turned, own, arrived, powers, scales, column_scale, embed_start
):
    crops, depth = other_embed.shape
    width = arrived.shape[1]
    quarter_width = own.shape[1] // 4
    tile = tile_width(quarter_width)
    tiles = quarter_width // tile
    begin, count = chunk_tiles(quarter_width)[chunk]
    quarter = depth // 4
    piece = jax.ShapeDtypeStruct((quarter, width), jnp.bfloat16)
    piece_spec = pl.BlockSpec((quarter, tile), lambda t, places: (0, t))
    starts = [] if embed_start is None else [embed_start]
    resident = pl.BlockSpec(memory_space=pltpu.VMEM)
    return pl.pallas_call(
        functools.partial(grads_body, embed_start is None),
        out_shape=(piece,) * 4 + (jax.ShapeDtypeStruct((crops, depth), jnp.float32),),
        grid_spec=pltpu.PrefetchScalarGridSpec(
            num_scalar_prefetch=1,
            grid=(count,),
            in_specs=[
                resident,
                resident,
                pl.BlockSpec((depth, tile), lambda t, places: (0, places[1] * tiles + begin + t)),
                pl.BlockSpec((depth, tile), lambda t, places: (0, t)),
                pl.BlockSpec(
                    (None, crops, tile),
                    lambda t, places: (
                        (places[0] * tiles + begin + t) // 2,
                        0,
                        lax.rem(begin + t, 2),
                    ),
                ),
                resident,
                resident,
                pl.BlockSpec((1, tile), lambda t, places: (0, begin + t)),
                *[resident for _ in starts],
            ],
            out_specs=[piece_spec] * 4 + [resident],
            scratch_shapes=[pltpu.VMEM((crops, tile), jnp.bfloat16)],
        ),
        cost_estimate=cost(
            6 * crops * depth * width,
            6 * depth * width + 4 * crops * width + 8 * crops * depth,
            crops * width,
        ),
        name="gradients",
    )(places, other_embed, turned, own, arrived, powers, *scales, column_scale, *starts)


def place_body(tiles, begin, tile, places, *refs):
    pieces, after, arrivals = refs[:4], refs[-2], refs[-1]
    width = pieces[0].shape[1]
    copies = []
    for place, piece in enumerate(pieces):
        start = pl.multiple_of((places[4 + place] * tiles + begin) * tile, tile)
        copies.append(
            pltpu.make_async_copy(piece, after.at[:, pl.ds(start, width)], arrivals.at[place])
        )
    for copy in copies:
        copy.start()
    for copy in copies:
        copy.wait()


def placed_pieces(places, chunk, pieces, before, block_width):
    rows, width = pieces[0].shape
    tile = tile_width(block_width // 4)
    tiles = block_width // 4 // tile
    begin, _ = chunk_tiles(block_width // 4)[chunk]
    operands = [places, *pieces] + ([] if before is None else [before])
    specs = [pl.BlockSpec(memory_space=pltpu.VMEM)] * 4
    if before is not None:
        specs = specs + [pl.BlockSpec(memory_space=pl.ANY)]
    return pl.pallas_call(
        functools.partial(place_body, tiles, begin, tile),
        out_shape=jax.ShapeDtypeStruct((rows, block_width), pieces[0].dtype),
        grid_spec=pltpu.PrefetchScalarGridSpec(
            num_scalar_prefetch=1,
            grid=(1,),
            in_specs=specs,
            out_specs=pl.BlockSpec(memory_space=pl.ANY),
            scratch_shapes=[pltpu.SemaphoreType.DMA((4,))],
        ),
        input_output_aliases={} if before is None else {5: 0},
        cost_estimate=cost(0, 16 * rows * width, 0),
        name="placed_pieces",
    )(*operands)


def swapped(value, *axes):
    if axes == ("role", "crop"):
        return lax.ppermute(value, axes, [(0, 3), (1, 2), (2, 1), (3, 0)])
    return lax.ppermute(value, axes[0], [(0, 1), (1, 0)])


def summands(value):
    axes = ("proto", "crop")
    count = lax.axis_size("proto") * lax.axis_size("crop")
    if count & (count - 1):
        return [lax.psum(value, axes)]
    parts = [value]
    stride = 1
    while stride < count:
        if stride > 1:
            parts = [functools.reduce(jnp.add, parts)]
        masks = [stride * k for k in (1, 2, 3) if stride * k < count]
        for mask in masks:
            pairs = [(place, place ^ mask) for place in range(count)]
            parts.append(lax.ppermute(parts[0], axes, pairs))
        stride *= 4
    return parts


def halving_masks(axis):
    count = lax.axis_size(axis)
    return [1 << bit for bit in range(count.bit_length() - 1)]


def is_power_of_two(count):
    return count & (count - 1) == 0


def flipped(value, axis, mask):
    return lax.ppermute(value, axis, [(p, p ^ mask) for p in range(lax.axis_size(axis))])


def bit_of(place, mask):
    return jnp.where((place & mask) != 0, 1, 0)


def scattered(value):
    count = lax.axis_size("proto")
    if not is_power_of_two(count):
        return lax.psum_scatter(value, ("crop", "proto"), scatter_dimension=0, tiled=True)
    width = value.shape[1]
    rows = value.shape[0] // 2 // count
    steps = [("crop", 1)] + [("proto", mask) for mask in halving_masks("proto")]
    for axis, mask in steps:
        bit = bit_of(lax.axis_index(axis), mask)
        low = value.shape[0] // 2 if axis == "crop" else rows
        halves = value.reshape(-1, 2, low, width)
        theirs = lax.dynamic_index_in_dim(halves, 1 - bit, 1, keepdims=False)
        mine = lax.dynamic_index_in_dim(halves, bit, 1, keepdims=False)
        got = flipped(theirs.reshape(-1, width), axis, mask)
        value = mine.reshape(-1, width) + got
    return value


def joined(mine, other, bit):
    return jnp.concatenate(
        [jnp.where(bit == 0, mine, other), jnp.where(bit == 0, other, mine)], axis=0
    )


def step(embeddings, weights):
    role_place = lax.axis_index("role")
    crop_place = lax.axis_index("crop")
    own_embed = embeddings[0]
    own_weight = weights[0]
    crops = 2 * own_embed.shape[0]
    depth = own_embed.shape[1]
    block_width = own_weight.shape[1]
    teaches = role_place == 0

    own_quarter = 2 * crop_place + role_place
    partner_quarter = 2 * crop_place + 1 - role_place
    order = [own_quarter, own_quarter ^ 2, own_quarter ^ 1, own_quarter ^ 3]
    places = jnp.stack([role_place, own_quarter, partner_quarter, crop_place] + order).astype(
        jnp.int32
    )

    crop_embed = swapped(own_embed, "crop")
    arrived = []
    for chunk in range(SLICED):
        sent = columns_of(places, own_weight, chunk)
        arrived.append(swapped(sent, "role"))
    proto_place = lax.axis_index("proto")
    spread = is_power_of_two(lax.axis_size("proto"))
    masks = halving_masks("proto") if spread else []
    part_rows = own_embed.shape[0] // lax.axis_size("proto") if spread else own_embed.shape[0]
    part_start = part_rows * proto_place if spread else 0
    role_embed = swapped(lax.dynamic_slice_in_dim(own_embed, part_start, part_rows), "role")
    got_embed = None
    if masks:
        got_embed = flipped(role_embed, "proto", masks[0])
    own_all = joined(own_embed, crop_embed, crop_place)

    scale = jnp.where(teaches, LOG2E / 0.07, LOG2E / 0.1).astype(jnp.float32).reshape(1)
    parts = []
    diagonal_embed = None
    for iteration in range(ITERS):
        if iteration == 0:
            row_sums, own_factor, partner_factor, powers, *columns = first_pass(
                places, scale, own_all, own_weight
            )
        else:
            row_sums, own_factor, partner_factor = later_pass(places, powers, parts)
        if iteration == 0:
            for chunk in range(SLICED, CHUNKS):
                arrived.append(swapped(columns[chunk - SLICED], "role"))
        parts = summands(row_sums)
        for place, mask in enumerate(masks):
            if min(place, ITERS - 1) != iteration:
                continue
            role_embed, got_embed, _ = lax.optimization_barrier((role_embed, got_embed, row_sums))
            role_embed = joined(role_embed, got_embed, bit_of(proto_place, mask))
            if place + 1 < len(masks):
                got_embed = flipped(role_embed, "proto", masks[place + 1])

        if iteration == ITERS - 1:
            diagonal_embed = swapped(role_embed, "crop")
    role_embed, diagonal_embed, own_all, _ = lax.optimization_barrier(
        (role_embed, diagonal_embed, own_all, row_sums)
    )
    other_all = joined(role_embed, diagonal_embed, crop_place)
    blocks = jnp.where(teaches, other_all, own_all).T.reshape(4, depth // 4, crops)
    turned = jnp.concatenate(
        [lax.dynamic_index_in_dim(blocks, place, 0, keepdims=False) for place in order], axis=0
    )

    got_factor = swapped(partner_factor, "role")
    inverse = 1.0 / functools.reduce(jnp.add, parts)
    got_inverse = swapped(inverse, "role")
    row_scale, inverse_sum, columns = final_scales(
        places, parts, got_inverse, own_factor, got_factor, (turned, other_all)
    )

    embed_part = None
    result = None
    for chunk in GRAD_ORDER:
        kept_piece, crop_piece, role_piece, diagonal_piece, embed_part = gradients(
            places,
            chunk,
            other_all,
            turned,
            own_weight,
            arrived[chunk],
            powers,
            (row_scale, inverse_sum),
            columns,
            embed_part,
        )
        diagonal_piece = swapped(diagonal_piece, "role", "crop")
        role_piece = swapped(role_piece, "role")
        crop_piece = swapped(crop_piece, "crop")
        pieces = (kept_piece, crop_piece, role_piece, diagonal_piece)
        result = placed_pieces(places, chunk, pieces, result, block_width)
    weight_block = result.reshape(1, 1, depth // 4, block_width)

    summed = scattered(embed_part)
    sides = summed.reshape(summed.shape[0], 2, depth // 2)
    theirs = lax.dynamic_index_in_dim(sides, 1 - role_place, 1, keepdims=False)
    mine = lax.dynamic_index_in_dim(sides, role_place, 1, keepdims=False)
    got_side = swapped(theirs, "role")
    embed_block = (mine + got_side).astype(jnp.bfloat16)[None]
    return (weight_block, embed_block)


def solution(mesh):
    placed = (P("role", "crop", None), P("role", None, "proto"))
    return jax.shard_map(
        step,
        mesh=mesh,
        in_specs=placed,
        out_specs=(P("crop", "role", None, "proto"), P("crop", "proto", "role")),
        check_vma=False,
    )
```

time: 409 us -> 436 us (1.066)
  waiting for transfers between devices: 133 us -> 193 us
  Pallas kernels: 207 us -> 174 us
  starting transfers between devices: 43.8 us -> 48.8 us
    ppermute x18 -> x21, waiting for transfers between devices: 77.9 us -> 144 us  [swapped(): return lax.ppermute(value, axes[0], [(0, 1), (1, 0)])]
    pallas_call x12 -> x15, Pallas kernels: 204 us -> 171 us  [the longest x5 66 us: gradients(): pl.pallas_call(functools.partial(grads_body, embed_start is None), out_sh...]
    ppermute x7, waiting for transfers between devices: 14 us -> 29.6 us  [flipped(): lax.ppermute(value, axis, [(p, p ^ mask) for p in range(lax.axis_size(axi...]
    ppermute x4 -> x5, waiting for transfers between devices: 24.7 us -> 10.8 us  [swapped(): return lax.ppermute(value, axes, [(0, 3), (1, 2), (2, 1), (3, 0)])]
    ppermute x18, waiting for transfers between devices: 16.2 us -> 8.45 us  [summands(): parts.append(lax.ppermute(parts[0], axes, pairs))]
    ppermute x18 -> x21, starting transfers between devices: 18.5 us -> 20.7 us  [swapped(): return lax.ppermute(value, axes[0], [(0, 1), (1, 0)])]
  transfers between devices with their start and end apart: 47 -> 51, of which waited for: 23 -> 17; matrix products, arithmetic and copies ran while one was open for 3% -> 2% of each run, Pallas kernels for 39% -> 38%
where the time goes in v1:
time: 436 us; the launch traced here: 435 us
  waiting for transfers between devices  193 us (44%)
  Pallas kernels  174 us (40%)
  starting transfers between devices  48.8 us (11%)
  other arithmetic  9.32 us (2%)
  local copies, waits for them, and re-layouts  8.06 us (2%)
    ppermute x21, waiting for transfers between devices, swapped(): return lax.ppermute(value, axes[0], [(0, 1), (1, 0)])  144 us
    pallas_call x5, Pallas kernels, gradients(): pl.pallas_call(functools.partial(grads_body, embed_start is None), out_sh...  66 us
    pallas_call x2, Pallas kernels, later_pass(): pl.pallas_call(functools.partial(later_body, len(parts), tiles), out_shap...  46.8 us
    pallas_call x1, Pallas kernels, first_pass(): pl.pallas_call(functools.partial(first_body, tiles), out_shape=shapes + [...  35.8 us
    ppermute x7, waiting for transfers between devices, flipped(): lax.ppermute(value, axis, [(p, p ^ mask) for p in range(lax.axis_size(axi...  29.6 us
    ppermute x21, starting transfers between devices, swapped(): return lax.ppermute(value, axes[0], [(0, 1), (1, 0)])  20.7 us
    ppermute x18, starting transfers between devices, summands(): parts.append(lax.ppermute(parts[0], axes, pairs))  19.5 us
    pallas_call x5, Pallas kernels, placed_pieces(): pl.pallas_call(functools.partial(place_body, tiles, begin, tile), out_sha...  16.3 us
  transfers between devices with their start and end apart: 51, of which 17 were waited for; matrix products, arithmetic and copies ran while one was open for 2% of the time, Pallas kernels for 38%

profile of v1, /device:TPU:0, one launch (start us, length us, event | category | flops | bytes accessed | tf_op | source)
XLA Modules:
  0.0 434.6 jit_solution(4641293892091028421)
XLA Ops:
  2.0 2.5 collective-permute-start
  11.2 35.8 %first_pass.1 = (f32[1,1024]{1,0:T(1,128)}, f32[1,8192]{1,0:T(1,128)}, f32[1,8192]{1,0:T(1,128)}, f32[16,1024,1024]{2,1,0:T(8,128)}, bf16[512,1024]{1,0:T(8,128)...) custom-call(s32[8]{0:T(128)} %stack.32.places, f32[1]{0:T(128)} %bitcast.8.scale, ...), custom_call_target="tpu_custom_call" | custom-call | flops 17179869184 | bytes 83886080 | tf_op jit(solution)/shard_map/first_pass/pallas_call | solution.py:223
  53.2 2.6 collective-permute-start.8
  56.0 3.9 columns_of.3
  62.1 23.4 %later_pass.2 = (f32[1,1024]{1,0:T(1,128)}, f32[1,8192]{1,0:T(1,128)}, f32[1,8192]{1,0:T(1,128)}) custom-call(s32[8]{0:T(128)} %stack.32.places, f32[16,1024,1024]{2,1,0:T(8,128)} %get-tuple-element.51.powers, f32[1,1024]{1,0:T(1,128)} %copy-done.20, f32[1,1024]{1,0:T(1,128)} %copy-done.23, f32[1,1024]{1,0:T(1,128)} %copy-done.24, f32[1,1024]{1,0:T(1,128)} %copy-done.26), custom_call_target="tpu_custom_call" | custom-call | flops 67108864 | bytes 67108864 | tf_op jit(solution)/shard_map/later_pass/pallas_call | solution.py:255
  92.7 2.5 collective-permute-start.14
  95.4 2.3 collective-permute-start.16
  101.4 23.4 %later_pass.3 = (f32[1,1024]{1,0:T(1,128)}, f32[1,8192]{1,0:T(1,128)}, f32[1,8192]{1,0:T(1,128)}) custom-call(s32[8]{0:T(128)} %stack.32.places, f32[16,1024,1024]{2,1,0:T(8,128)} %get-tuple-element.51.powers, f32[1,1024]{1,0:T(1,128)} %copy-done.21, f32[1,1024]{1,0:T(1,128)} %copy-done.25, f32[1,1024]{1,0:T(1,128)} %copy-done.27, f32[1,1024]{1,0:T(1,128)} %copy-done.28), custom_call_target="tpu_custom_call" | custom-call | flops 67108864 | bytes 67108864 | tf_op jit(solution)/shard_map/later_pass/pallas_call | solution.py:255
  129.7 3.1 collective-permute-start.23
  134.0 2.5 columns_of.2
  142.9 108.5 %collective-permute-done.25.refs_4_ = f32[1,1024]{1,0:T(1,128)S(1)} collective-permute-done((f32[1,1024]{1,0:T(1,128)S(1)}, f32[1,1024]{1,0:T(1,128)S(1)}, u32[]{:S(2)}, u32[]{:S(2)}) %collective-permute-start.25) | collective-permute-done | bytes 4128 | tf_op jit(solution)/shard_map/ppermute | solution.py:445
  252.9 2.3 collective-permute-done.26.refs_6_
  255.9 2.8 final_scales.1
  259.7 10.0 %gradients.5 = (bf16[128,1024]{1,0:T(8,128)(2,1)}, bf16[128,1024]{1,0:T(8,128)(2,1)}, bf16[128,1024]{1,0:T(8,128)(2,1)}, bf16[128,1024]{1,0:T(8,128)(2,1)}, f32[1024,512]{1,0:T(8,128)}) custom-call(s32[8]{0:T(128)} %stack.32.places, bf16[1024,512]{1,0:T(8,128)(2,1)} %get-tuple-element.101.refs_8_.other_embed, ...), custom_call_target="tpu_custom_call" | custom-call | flops 3221225472 | bytes 11534336 | tf_op jit(solution)/shard_map/gradients/pallas_call | solution.py:366
  269.7 17.5 %gradients.6 = (bf16[128,2560]{1,0:T(8,128)(2,1)}, bf16[128,2560]{1,0:T(8,128)(2,1)}, bf16[128,2560]{1,0:T(8,128)(2,1)}, bf16[128,2560]{1,0:T(8,128)(2,1)}, f32[1024,512]{1,0:T(8,128)}) custom-call(s32[8]{0:T(128)} %stack.32.places, bf16[1024,512]{1,0:T(8,128)(2,1)} %get-tuple-element.101.refs_8_.other_embed, ...), custom_call_target="tpu_custom_call" | custom-call | flops 8053063680 | bytes 22544384 | tf_op jit(solution)/shard_map/gradients/pallas_call | solution.py:366
  287.2 15.2 %gradients.7 = (bf16[128,2048]{1,0:T(8,128)(2,1)}, bf16[128,2048]{1,0:T(8,128)(2,1)}, bf16[128,2048]{1,0:T(8,128)(2,1)}, bf16[128,2048]{1,0:T(8,128)(2,1)}, f32[1024,512]{1,0:T(8,128)}) custom-call(s32[8]{0:T(128)} %stack.32.places, bf16[1024,512]{1,0:T(8,128)(2,1)} %get-tuple-element.101.refs_8_.other_embed, ...), custom_call_target="tpu_custom_call" | custom-call | flops 6442450944 | bytes 18874368 | tf_op jit(solution)/shard_map/gradients/pallas_call | solution.py:366
  302.4 15.4 %gradients.8 = (bf16[128,2048]{1,0:T(8,128)(2,1)}, bf16[128,2048]{1,0:T(8,128)(2,1)}, bf16[128,2048]{1,0:T(8,128)(2,1)}, bf16[128,2048]{1,0:T(8,128)(2,1)}, f32[1024,512]{1,0:T(8,128)}) custom-call(s32[8]{0:T(128)} %stack.32.places, bf16[1024,512]{1,0:T(8,128)(2,1)} %get-tuple-element.101.refs_8_.other_embed, ...), custom_call_target="tpu_custom_call" | custom-call | flops 6442450944 | bytes 18874368 | tf_op jit(solution)/shard_map/gradients/pallas_call | solution.py:366
  318.6 8.0 %gradients.9 = (bf16[128,512]{1,0:T(8,128)(2,1)}, bf16[128,512]{1,0:T(8,128)(2,1)}, bf16[128,512]{1,0:T(8,128)(2,1)}, bf16[128,512]{1,0:T(8,128)(2,1)}, f32[1024,512]{1,0:T(8,128)}) custom-call(s32[8]{0:T(128)} %stack.32.places, bf16[1024,512]{1,0:T(8,128)(2,1)} %get-tuple-element.101.refs_8_.other_embed, ...), custom_call_target="tpu_custom_call" | custom-call | flops 1610612736 | bytes 7864320 | tf_op jit(solution)/shard_map/gradients/pallas_call | solution.py:366
  328.0 2.8 collective-permute-done.46
  333.5 2.6 collective-permute-start.44
  336.4 10.0 %collective-permute-done.47 = f32[256,512]{1,0:T(8,128)S(1)} collective-permute-done((f32[256,512]{1,0:T(8,128)S(1)}, f32[256,512]{1,0:T(8,128)S(1)}, u32[]{:S(2)}, u32[]{:S(2)}) %collective-permute-start.47) | collective-permute-done | bytes 524320 | tf_op jit(solution)/shard_map/ppermute | solution.py:476
  346.4 2.6 collective-permute-start.38
  350.0 7.7 %collective-permute-done.48 = f32[128,512]{1,0:T(8,128)S(1)} collective-permute-done((f32[128,512]{1,0:T(8,128)S(1)}, f32[128,512]{1,0:T(8,128)S(1)}, u32[]{:S(2)}, u32[]{:S(2)}) %collective-permute-start.48) | collective-permute-done | bytes 262176 | tf_op jit(solution)/shard_map/ppermute | solution.py:476
  359.6 2.4 collective-permute-done.38.refs_2_
  362.1 10.8 %collective-permute-done.39.refs_3_ = bf16[128,2048]{1,0:T(8,128)(2,1)} collective-permute-done((bf16[128,2048]{1,0:T(8,128)(2,1)}, bf16[128,2048]{1,0:T(8,128)(2,1)}, u32[]{:S(2)}, u32[]{:S(2)}) %collective-permute-start.39) | collective-permute-done | bytes 524320 | tf_op jit(solution)/shard_map/ppermute | solution.py:444
  373.5 9.1 %collective-permute-done.49 = f32[64,512]{1,0:T(8,128)S(1)} collective-permute-done((f32[64,512]{1,0:T(8,128)S(1)}, f32[64,512]{1,0:T(8,128)S(1)}, u32[]{:S(2)}, u32[]{:S(2)}) %collective-permute-start.49) | collective-permute-done | bytes 131104 | tf_op jit(solution)/shard_map/ppermute | solution.py:476
  384.1 28.6 %collective-permute-done.35.refs_2_ = bf16[128,2048]{1,0:T(8,128)(2,1)} collective-permute-done((bf16[128,2048]{1,0:T(8,128)(2,1)}, bf16[128,2048]{1,0:T(8,128)(2,1)}, u32[]{:S(2)}, u32[]{:S(2)}) %collective-permute-start.35) | collective-permute-done | bytes 524320 | tf_op jit(solution)/shard_map/ppermute | solution.py:445
  416.8 2.8 placed_pieces.5.refs_4_
  419.7 3.9 placed_pieces.6.refs_4_
  423.6 3.5 placed_pieces.7.refs_4_
  427.1 3.5 placed_pieces.8.refs_4_
  431.4 2.6 placed_pieces.9
  (181 shorter events, 58.6 us)
Async XLA Ops:
  0.6 8.4 %collective-permute-start.2 = (bf16[512,512]{1,0:T(8,128)(2,1)}, bf16[512,512]{1,0:T(8,128)(2,1)S(1)}, u32[]{:S(2)}, u32[]{:S(2)}) collective-permute-start(bf16[512,512]{1,0:T(8,128)(2,1)} %bitcast.71), channel_id=1, source_target_pairs={{0,1},{1,0},{2,3},{3,2},{4,5},{5,4},{6,7},{7,6},{8,9},{9,8},{10,11... | collective-permute-start | bytes 1572872 | tf_op jit(solution)/shard_map/ppermute | solution.py:445
  7.3 41.5 %collective-permute-start.1 = (bf16[64,512]{1,0:T(8,128)(2,1)S(1)}, bf16[64,512]{1,0:T(8,128)(2,1)S(1)}, u32[]{:S(2)}, u32[]{:S(2)}) collective-permute-start(bf16[64,512]{1,0:T(8,128)(2,1)S(1)} %collective-permute-done), channel_id=1, source_target_pairs={{0,2},{2,0},{4,6},{6,4},{8,10},{10,8},{12,14},{14,12},{1,3},{3,1},... | collective-permute-start | bytes 196616 | tf_op jit(solution)/shard_map/ppermute | solution.py:476
  48.9 36.7 %collective-permute-start.3 = (bf16[128,512]{1,0:T(8,128)(2,1)S(1)}, bf16[128,512]{1,0:T(8,128)(2,1)S(1)}, u32[]{:S(2)}, u32[]{:S(2)}) collective-permute-start(bf16[128,512]{1,0:T(8,128)(2,1)S(1)} %pad_maximum_fusion.5), channel_id=1, source_target_pairs={{0,4},{2,6},{4,0},{6,2},{8,12},{10,14},{12,8},{14,10},{1,5},{3,7},... | collective-permute-start | bytes 393224 | tf_op jit(solution)/shard_map/ppermute | solution.py:476
  51.6 10.0 %collective-permute-start.7 = (f32[1,1024]{1,0:T(1,128)S(1)}, f32[1,1024]{1,0:T(1,128)S(1)}, u32[]{:S(2)}, u32[]{:S(2)}) collective-permute-start(f32[1,1024]{1,0:T(1,128)S(1)} %add_add_fusion.2.refs_0_), channel_id=1, source_target_pairs={{0,4},{1,5},{2,6},{3,7},{4,0},{5,1},{6,2},{7,3},{8,12},{9,13},{10,... | collective-permute-start | bytes 12296 | tf_op jit(solution)/shard_map/ppermute | solution.py:461
  53.2 8.3 %collective-permute-start.8 = (f32[1,1024]{1,0:T(1,128)S(1)}, f32[1,1024]{1,0:T(1,128)S(1)}, u32[]{:S(2)}, u32[]{:S(2)}) collective-permute-start(f32[1,1024]{1,0:T(1,128)S(1)} %add_add_fusion.2.refs_0_), channel_id=1, source_target_pairs={{0,8},{1,9},{2,10},{3,11},{4,12},{5,13},{6,14},{7,15},{8,0},{9,1},... | collective-permute-start | bytes 12296 | tf_op jit(solution)/shard_map/ppermute | solution.py:461
  59.9 209.7 %collective-permute-start.29 = (bf16[512,2560]{1,0:T(8,128)(2,1)}, bf16[512,2560]{1,0:T(8,128)(2,1)}, u32[]{:S(2)}, u32[]{:S(2)}) collective-permute-start(bf16[512,2560]{1,0:T(8,128)(2,1)} %columns_of.3), channel_id=1, source_target_pairs={{0,16},{16,0},{1,17},{17,1},{2,18},{18,2},{3,19},{19,3},{4,20},{20... | collective-permute-start | bytes 7864328 | tf_op jit(solution)/shard_map/ppermute | solution.py:445
  85.6 39.2 %collective-permute-start.10 = (bf16[256,512]{1,0:T(8,128)(2,1)S(1)}, bf16[256,512]{1,0:T(8,128)(2,1)S(1)}, u32[]{:S(2)}, u32[]{:S(2)}) collective-permute-start(bf16[256,512]{1,0:T(8,128)(2,1)S(1)} %pad_maximum_fusion.4), channel_id=1, source_target_pairs={{0,8},{2,10},{4,12},{6,14},{8,0},{10,2},{12,4},{14,6},{1,9},{3,11}... | collective-permute-start | bytes 786440 | tf_op jit(solution)/shard_map/ppermute | solution.py:476
  125.0 14.3 %collective-permute-start.17 = (bf16[512,512]{1,0:T(8,128)(2,1)S(1)}, bf16[512,512]{1,0:T(8,128)(2,1)S(1)}, u32[]{:S(2)}, u32[]{:S(2)}) collective-permute-start(bf16[512,512]{1,0:T(8,128)(2,1)S(1)} %pad_maximum_fusion.3), channel_id=1, source_target_pairs={{0,1},{1,0},{2,3},{3,2},{4,5},{5,4},{6,7},{7,6},{8,9},{9,8},{10,11... | collective-permute-start | bytes 1572872 | tf_op jit(solution)/shard_map/ppermute | solution.py:445
  136.6 122.1 %collective-permute-start.30 = (bf16[512,1024]{1,0:T(8,128)(2,1)}, bf16[512,1024]{1,0:T(8,128)(2,1)S(1)}, u32[]{:S(2)}, u32[]{:S(2)}) collective-permute-start(bf16[512,1024]{1,0:T(8,128)(2,1)} %get-tuple-element.68), channel_id=1, source_target_pairs={{0,16},{16,0},{1,17},{17,1},{2,18},{18,2},{3,19},{19,3},{4,20},{20... | collective-permute-start | bytes 3145736 | tf_op jit(solution)/shard_map/ppermute | solution.py:445
  137.2 150.0 %collective-permute-start.28 = (bf16[512,2048]{1,0:T(8,128)(2,1)}, bf16[512,2048]{1,0:T(8,128)(2,1)}, u32[]{:S(2)}, u32[]{:S(2)}) collective-permute-start(bf16[512,2048]{1,0:T(8,128)(2,1)} %get-tuple-element.67), channel_id=1, source_target_pairs={{0,16},{16,0},{1,17},{17,1},{2,18},{18,2},{3,19},{19,3},{4,20},{20... | collective-permute-start | bytes 6291464 | tf_op jit(solution)/shard_map/ppermute | solution.py:445
  138.7 163.7 %collective-permute-start.27 = (bf16[512,2048]{1,0:T(8,128)(2,1)}, bf16[512,2048]{1,0:T(8,128)(2,1)}, u32[]{:S(2)}, u32[]{:S(2)}) collective-permute-start(bf16[512,2048]{1,0:T(8,128)(2,1)} %get-tuple-element.66), channel_id=1, source_target_pairs={{0,16},{16,0},{1,17},{17,1},{2,18},{18,2},{3,19},{19,3},{4,20},{20... | collective-permute-start | bytes 6291464 | tf_op jit(solution)/shard_map/ppermute | solution.py:445
  139.3 112.1 %collective-permute-start.25 = (f32[1,1024]{1,0:T(1,128)S(1)}, f32[1,1024]{1,0:T(1,128)S(1)}, u32[]{:S(2)}, u32[]{:S(2)}) collective-permute-start(f32[1,1024]{1,0:T(1,128)S(1)} %add_divide_fusion), channel_id=1, source_target_pairs={{0,16},{16,0},{1,17},{17,1},{2,18},{18,2},{3,19},{19,3},{4,20},{20... | collective-permute-start | bytes 12296 | tf_op jit(solution)/shard_map/ppermute | solution.py:445
  255.3 62.5 %collective-permute-start.18 = (bf16[512,512]{1,0:T(8,128)(2,1)}, bf16[512,512]{1,0:T(8,128)(2,1)S(1)}, u32[]{:S(2)}, u32[]{:S(2)}) collective-permute-start(bf16[512,512]{1,0:T(8,128)(2,1)} %columns_of.2), channel_id=1, source_target_pairs={{0,16},{16,0},{1,17},{17,1},{2,18},{18,2},{3,19},{19,3},{4,20},{20... | collective-permute-start | bytes 1572872 | tf_op jit(solution)/shard_map/ppermute | solution.py:445
  332.4 14.0 %collective-permute-start.47 = (f32[256,512]{1,0:T(8,128)S(1)}, f32[256,512]{1,0:T(8,128)S(1)}, u32[]{:S(2)}, u32[]{:S(2)}) collective-permute-start(f32[256,512]{1,0:T(8,128)S(1)} %bitcast.72), channel_id=1, source_target_pairs={{0,2},{2,0},{4,6},{6,4},{8,10},{10,8},{12,14},{14,12},{1,3},{3,1},... | collective-permute-start | bytes 1572872 | tf_op jit(solution)/shard_map/ppermute | solution.py:476
  333.5 15.7 %collective-permute-start.43 = (bf16[128,1024]{1,0:T(8,128)(2,1)S(1)}, bf16[128,1024]{1,0:T(8,128)(2,1)S(1)}, u32[]{:S(2)}, u32[]{:S(2)}) collective-permute-start(bf16[128,1024]{1,0:T(8,128)(2,1)S(1)} %copy-done.30), channel_id=1, source_target_pairs={{0,1},{1,0},{2,3},{3,2},{4,5},{5,4},{6,7},{7,6},{8,9},{9,8},{10,11... | collective-permute-start | bytes 786440 | tf_op jit(solution)/shard_map/ppermute | solution.py:445
  333.5 15.8 %collective-permute-start.44 = (bf16[128,1024]{1,0:T(8,128)(2,1)}, bf16[128,1024]{1,0:T(8,128)(2,1)S(1)}, u32[]{:S(2)}, u32[]{:S(2)}) collective-permute-start(bf16[128,1024]{1,0:T(8,128)(2,1)} %get-tuple-element.91), channel_id=1, source_target_pairs={{0,16},{16,0},{1,17},{17,1},{2,18},{18,2},{3,19},{19,3},{4,20},{20... | collective-permute-start | bytes 786440 | tf_op jit(solution)/shard_map/ppermute | solution.py:445
  336.1 13.3 %collective-permute-start.45 = (bf16[128,1024]{1,0:T(8,128)(2,1)}, bf16[128,1024]{1,0:T(8,128)(2,1)S(1)}, u32[]{:S(2)}, u32[]{:S(2)}) collective-permute-start(bf16[128,1024]{1,0:T(8,128)(2,1)} %get-tuple-element.92), channel_id=1, source_target_pairs={{0,17},{1,16},{16,1},{17,0},{2,19},{3,18},{18,3},{19,2},{4,21},{5,... | collective-permute-start | bytes 786440 | tf_op jit(solution)/shard_map/ppermute | solution.py:444
  336.3 13.3 %collective-permute-start.37 = (bf16[128,2048]{1,0:T(8,128)(2,1)}, bf16[128,2048]{1,0:T(8,128)(2,1)S(1)}, u32[]{:S(2)}, u32[]{:S(2)}) collective-permute-start(bf16[128,2048]{1,0:T(8,128)(2,1)} %get-tuple-element.82), channel_id=1, source_target_pairs={{0,1},{1,0},{2,3},{3,2},{4,5},{5,4},{6,7},{7,6},{8,9},{9,8},{10,11... | collective-permute-start | bytes 1572872 | tf_op jit(solution)/shard_map/ppermute | solution.py:445
  346.4 15.6 %collective-permute-start.38 = (bf16[128,2048]{1,0:T(8,128)(2,1)}, bf16[128,2048]{1,0:T(8,128)(2,1)S(1)}, u32[]{:S(2)}, u32[]{:S(2)}) collective-permute-start(bf16[128,2048]{1,0:T(8,128)(2,1)} %get-tuple-element.83), channel_id=1, source_target_pairs={{0,16},{16,0},{1,17},{17,1},{2,18},{18,2},{3,19},{19,3},{4,20},{20... | collective-permute-start | bytes 1572872 | tf_op jit(solution)/shard_map/ppermute | solution.py:445
  349.2 23.8 %collective-permute-start.39 = (bf16[128,2048]{1,0:T(8,128)(2,1)}, bf16[128,2048]{1,0:T(8,128)(2,1)}, u32[]{:S(2)}, u32[]{:S(2)}) collective-permute-start(bf16[128,2048]{1,0:T(8,128)(2,1)} %get-tuple-element.84), channel_id=1, source_target_pairs={{0,17},{1,16},{16,1},{17,0},{2,19},{3,18},{18,3},{19,2},{4,21},{5,... | collective-permute-start | bytes 1572872 | tf_op jit(solution)/shard_map/ppermute | solution.py:444
  349.3 8.4 %collective-permute-start.48 = (f32[128,512]{1,0:T(8,128)S(1)}, f32[128,512]{1,0:T(8,128)S(1)}, u32[]{:S(2)}, u32[]{:S(2)}) collective-permute-start(f32[128,512]{1,0:T(8,128)S(1)} %bitcast.73), channel_id=1, source_target_pairs={{0,4},{2,6},{4,0},{6,2},{8,12},{10,14},{12,8},{14,10},{1,5},{3,7},... | collective-permute-start | bytes 786440 | tf_op jit(solution)/shard_map/ppermute | solution.py:476
  349.4 23.5 %collective-permute-start.34 = (bf16[128,2048]{1,0:T(8,128)(2,1)}, bf16[128,2048]{1,0:T(8,128)(2,1)}, u32[]{:S(2)}, u32[]{:S(2)}) collective-permute-start(bf16[128,2048]{1,0:T(8,128)(2,1)} %get-tuple-element.78), channel_id=1, source_target_pairs={{0,1},{1,0},{2,3},{3,2},{4,5},{5,4},{6,7},{7,6},{8,9},{9,8},{10,11... | collective-permute-start | bytes 1572872 | tf_op jit(solution)/shard_map/ppermute | solution.py:445
  349.6 63.1 %collective-permute-start.40 = (bf16[128,2560]{1,0:T(8,128)(2,1)}, bf16[128,2560]{1,0:T(8,128)(2,1)S(1)}, u32[]{:S(2)}, u32[]{:S(2)}) collective-permute-start(bf16[128,2560]{1,0:T(8,128)(2,1)} %get-tuple-element.86), channel_id=1, source_target_pairs={{0,1},{1,0},{2,3},{3,2},{4,5},{5,4},{6,7},{7,6},{8,9},{9,8},{10,11... | collective-permute-start | bytes 1966088 | tf_op jit(solution)/shard_map/ppermute | solution.py:445
  357.7 57.1 %collective-permute-start.41 = (bf16[128,2560]{1,0:T(8,128)(2,1)}, bf16[128,2560]{1,0:T(8,128)(2,1)S(1)}, u32[]{:S(2)}, u32[]{:S(2)}) collective-permute-start(bf16[128,2560]{1,0:T(8,128)(2,1)} %get-tuple-element.87), channel_id=1, source_target_pairs={{0,16},{16,0},{1,17},{17,1},{2,18},{18,2},{3,19},{19,3},{4,20},{20... | collective-permute-start | bytes 1966088 | tf_op jit(solution)/shard_map/ppermute | solution.py:445
  362.1 53.0 %collective-permute-start.42 = (bf16[128,2560]{1,0:T(8,128)(2,1)}, bf16[128,2560]{1,0:T(8,128)(2,1)S(1)}, u32[]{:S(2)}, u32[]{:S(2)}) collective-permute-start(bf16[128,2560]{1,0:T(8,128)(2,1)} %get-tuple-element.88), channel_id=1, source_target_pairs={{0,17},{1,16},{16,1},{17,0},{2,19},{3,18},{18,3},{19,2},{4,21},{5,... | collective-permute-start | bytes 1966088 | tf_op jit(solution)/shard_map/ppermute | solution.py:444
  372.9 39.8 %collective-permute-start.35 = (bf16[128,2048]{1,0:T(8,128)(2,1)}, bf16[128,2048]{1,0:T(8,128)(2,1)}, u32[]{:S(2)}, u32[]{:S(2)}) collective-permute-start(bf16[128,2048]{1,0:T(8,128)(2,1)} %get-tuple-element.79), channel_id=1, source_target_pairs={{0,16},{16,0},{1,17},{17,1},{2,18},{18,2},{3,19},{19,3},{4,20},{20... | collective-permute-start | bytes 1572872 | tf_op jit(solution)/shard_map/ppermute | solution.py:445
  373.0 9.7 %collective-permute-start.49 = (f32[64,512]{1,0:T(8,128)S(1)}, f32[64,512]{1,0:T(8,128)S(1)}, u32[]{:S(2)}, u32[]{:S(2)}) collective-permute-start(f32[64,512]{1,0:T(8,128)S(1)} %dynamic-slice_bitcast_fusion.5), channel_id=1, source_target_pairs={{0,8},{2,10},{4,12},{6,14},{8,0},{10,2},{12,4},{14,6},{1,9},{3,11}... | collective-permute-start | bytes 393224 | tf_op jit(solution)/shard_map/ppermute | solution.py:476
  382.6 44.5 %collective-permute-start.36 = (bf16[128,2048]{1,0:T(8,128)(2,1)}, bf16[128,2048]{1,0:T(8,128)(2,1)}, u32[]{:S(2)}, u32[]{:S(2)}) collective-permute-start(bf16[128,2048]{1,0:T(8,128)(2,1)} %get-tuple-element.80), channel_id=1, source_target_pairs={{0,17},{1,16},{16,1},{17,0},{2,19},{3,18},{18,3},{19,2},{4,21},{5,... | collective-permute-start | bytes 1572872 | tf_op jit(solution)/shard_map/ppermute | solution.py:444
  412.7 18.0 %collective-permute-start.31 = (bf16[128,512]{1,0:T(8,128)(2,1)}, bf16[128,512]{1,0:T(8,128)(2,1)S(1)}, u32[]{:S(2)}, u32[]{:S(2)}) collective-permute-start(bf16[128,512]{1,0:T(8,128)(2,1)} %get-tuple-element.74), channel_id=1, source_target_pairs={{0,1},{1,0},{2,3},{3,2},{4,5},{5,4},{6,7},{7,6},{8,9},{9,8},{10,11... | collective-permute-start | bytes 393224 | tf_op jit(solution)/shard_map/ppermute | solution.py:445
  412.7 18.0 %collective-permute-start.32 = (bf16[128,512]{1,0:T(8,128)(2,1)}, bf16[128,512]{1,0:T(8,128)(2,1)S(1)}, u32[]{:S(2)}, u32[]{:S(2)}) collective-permute-start(bf16[128,512]{1,0:T(8,128)(2,1)} %get-tuple-element.75), channel_id=1, source_target_pairs={{0,16},{16,0},{1,17},{17,1},{2,18},{18,2},{3,19},{19,3},{4,20},{20... | collective-permute-start | bytes 393224 | tf_op jit(solution)/shard_map/ppermute | solution.py:445
  414.8 15.9 %collective-permute-start.33 = (bf16[128,512]{1,0:T(8,128)(2,1)}, bf16[128,512]{1,0:T(8,128)(2,1)}, u32[]{:S(2)}, u32[]{:S(2)}) collective-permute-start(bf16[128,512]{1,0:T(8,128)(2,1)} %get-tuple-element.76), channel_id=1, source_target_pairs={{0,17},{1,16},{16,1},{17,0},{2,19},{3,18},{18,3},{19,2},{4,21},{5,... | collective-permute-start | bytes 393224 | tf_op jit(solution)/shard_map/ppermute | solution.py:444
  415.1 18.9 %collective-permute-start.50 = (f32[64,256]{1,0:T(8,128)S(1)}, f32[64,256]{1,0:T(8,128)S(1)}, u32[]{:S(2)}, u32[]{:S(2)}) collective-permute-start(f32[64,256]{1,0:T(8,128)S(1)} %bitcast.74), channel_id=1, source_target_pairs={{0,16},{16,0},{1,17},{17,1},{2,18},{18,2},{3,19},{19,3},{4,20},{20... | collective-permute-start | bytes 196616 | tf_op jit(solution)/shard_map/ppermute | solution.py:445
  (51 other events, 436.9 us)

commit v2 on v1

--- a/solution.py
+++ b/solution.py
@@ -56,15 +56,20 @@
     return jnp.concatenate([value] * (width // value.shape[1]), axis=1)
 
 
-def columns_body(tile, begin, places, matrix, target, arrived):
+def quarter_of(role_place, crop_place):
+    return 2 * crop_place + role_place
+
+
+def columns_body(tile, begin, matrix, target, arrived):
     width = target.shape[1]
-    start = pl.multiple_of(places[2] * (matrix.shape[1] // 4) + begin * tile, tile)
+    partner = quarter_of(1 - lax.axis_index("role"), lax.axis_index("crop"))
+    start = pl.multiple_of(partner * (matrix.shape[1] // 4) + begin * tile, tile)
     copy = pltpu.make_async_copy(matrix.at[:, pl.ds(start, width)], target, arrived)
     copy.start()
     copy.wait()
 
 
-def columns_of(places, matrix, chunk):
+def columns_of(matrix, chunk):
     depth = matrix.shape[0]
     quarter_width = matrix.shape[1] // 4
     tile = tile_width(quarter_width)
@@ -73,16 +78,12 @@
     return pl.pallas_call(
         functools.partial(columns_body, tile, begin),
         out_shape=jax.ShapeDtypeStruct((depth, width), matrix.dtype),
-        grid_spec=pltpu.PrefetchScalarGridSpec(
-            num_scalar_prefetch=1,
-            grid=(1,),
-            in_specs=[pl.BlockSpec(memory_space=pl.ANY)],
-            out_specs=pl.BlockSpec(memory_space=pltpu.VMEM),
-            scratch_shapes=[pltpu.SemaphoreType.DMA],
-        ),
+        in_specs=[pl.BlockSpec(memory_space=pl.ANY)],
+        out_specs=pl.BlockSpec(memory_space=pltpu.VMEM),
+        scratch_shapes=[pltpu.SemaphoreType.DMA],
         cost_estimate=cost(0, 4 * depth * width, 0),
         name="columns_of",
-    )(places, matrix)
+    )(matrix)
 
 
 def reciprocal_rows(parts, crops):
@@ -399,12 +400,18 @@
     )(places, other_embed, turned, own, arrived, powers, *scales, column_scale, *starts)
 
 
-def place_body(tiles, begin, tile, places, *refs):
+def place_body(tiles, begin, tile, *refs):
     pieces, after, arrivals = refs[:4], refs[-2], refs[-1]
     width = pieces[0].shape[1]
+    role_place, crop_place = lax.axis_index("role"), lax.axis_index("crop")
+    quarters = [
+        quarter_of(role, crop)
+        for role in (role_place, 1 - role_place)
+        for crop in (crop_place, 1 - crop_place)
+    ]
     copies = []
-    for place, piece in enumerate(pieces):
-        start = pl.multiple_of((places[4 + place] * tiles + begin) * tile, tile)
+    for place, (quarter, piece) in enumerate(zip(quarters, pieces)):
+        start = pl.multiple_of((quarter * tiles + begin) * tile, tile)
         copies.append(
             pltpu.make_async_copy(piece, after.at[:, pl.ds(start, width)], arrivals.at[place])
         )
@@ -414,26 +421,22 @@
         copy.wait()
 
 
-def placed_pieces(places, chunk, pieces, before, block_width):
+def placed_pieces(chunk, pieces, before, block_width):
     rows, width = pieces[0].shape
     tile = tile_width(block_width // 4)
     tiles = block_width // 4 // tile
     begin, _ = chunk_tiles(block_width // 4)[chunk]
-    operands = [places, *pieces] + ([] if before is None else [before])
+    operands = [*pieces] + ([] if before is None else [before])
     specs = [pl.BlockSpec(memory_space=pltpu.VMEM)] * 4
     if before is not None:
         specs = specs + [pl.BlockSpec(memory_space=pl.ANY)]
     return pl.pallas_call(
         functools.partial(place_body, tiles, begin, tile),
         out_shape=jax.ShapeDtypeStruct((rows, block_width), pieces[0].dtype),
-        grid_spec=pltpu.PrefetchScalarGridSpec(
-            num_scalar_prefetch=1,
-            grid=(1,),
-            in_specs=specs,
-            out_specs=pl.BlockSpec(memory_space=pl.ANY),
-            scratch_shapes=[pltpu.SemaphoreType.DMA((4,))],
-        ),
-        input_output_aliases={} if before is None else {5: 0},
+        in_specs=specs,
+        out_specs=pl.BlockSpec(memory_space=pl.ANY),
+        scratch_shapes=[pltpu.SemaphoreType.DMA((4,))],
+        input_output_aliases={} if before is None else {4: 0},
         cost_estimate=cost(0, 16 * rows * width, 0),
         name="placed_pieces",
     )(*operands)
@@ -514,17 +517,15 @@
     block_width = own_weight.shape[1]
     teaches = role_place == 0
 
-    own_quarter = 2 * crop_place + role_place
-    partner_quarter = 2 * crop_place + 1 - role_place
+    own_quarter = quarter_of(role_place, crop_place)
+    partner_quarter = quarter_of(1 - role_place, crop_place)
     order = [own_quarter, own_quarter ^ 2, own_quarter ^ 1, own_quarter ^ 3]
-    places = jnp.stack([role_place, own_quarter, partner_quarter, crop_place] + order).astype(
-        jnp.int32
-    )
+    places = jnp.stack([role_place, own_quarter, partner_quarter, crop_place]).astype(jnp.int32)
 
     crop_embed = swapped(own_embed, "crop")
     arrived = []
     for chunk in range(SLICED):
-        sent = columns_of(places, own_weight, chunk)
+        sent = columns_of(own_weight, chunk)
         arrived.append(swapped(sent, "role"))
     proto_place = lax.axis_index("proto")
     spread = is_power_of_two(lax.axis_size("proto"))
@@ -532,9 +533,6 @@
     part_rows = own_embed.shape[0] // lax.axis_size("proto") if spread else own_embed.shape[0]
     part_start = part_rows * proto_place if spread else 0
     role_embed = swapped(lax.dynamic_slice_in_dim(own_embed, part_start, part_rows), "role")
-    got_embed = None
-    if masks:
-        got_embed = flipped(role_embed, "proto", masks[0])
     own_all = joined(own_embed, crop_embed, crop_place)
 
     scale = jnp.where(teaches, LOG2E / 0.07, LOG2E / 0.1).astype(jnp.float32).reshape(1)
@@ -552,12 +550,11 @@
                 arrived.append(swapped(columns[chunk - SLICED], "role"))
         parts = summands(row_sums)
         for place, mask in enumerate(masks):
-            if min(place, ITERS - 1) != iteration:
+            if min(max(place - 1, 0), ITERS - 1) != iteration:
                 continue
-            role_embed, got_embed, _ = lax.optimization_barrier((role_embed, got_embed, row_sums))
+            role_embed, _ = lax.optimization_barrier((role_embed, row_sums))
+            got_embed = flipped(role_embed, "proto", mask)
             role_embed = joined(role_embed, got_embed, bit_of(proto_place, mask))
-            if place + 1 < len(masks):
-                got_embed = flipped(role_embed, "proto", masks[place + 1])
 
         if iteration == ITERS - 1:
             diagonal_embed = swapped(role_embed, "crop")
@@ -596,7 +593,7 @@
         role_piece = swapped(role_piece, "role")
         crop_piece = swapped(crop_piece, "crop")
         pieces = (kept_piece, crop_piece, role_piece, diagonal_piece)
-        result = placed_pieces(places, chunk, pieces, result, block_width)
+        result = placed_pieces(chunk, pieces, result, block_width)
     weight_block = result.reshape(1, 1, depth // 4, block_width)
 
     summed = scattered(embed_part)

time: 436 us -> 437 us (level)
  waiting for transfers between devices: 193 us -> 202 us
    ppermute x7, waiting for transfers between devices: 29.6 us -> 42 us  [flipped(): lax.ppermute(value, axis, [(p, p ^ mask) for p in range(lax.axis_size(axi...]
  transfers between devices with their start and end apart: 51 -> 51, of which waited for: 17 -> 17; matrix products, arithmetic and copies ran while one was open for 2% -> 2% of each run, Pallas kernels for 38% -> 37%
where the time goes in v2:
time: 437 us; the launch traced here: 435 us
  waiting for transfers between devices  202 us (46%)
  Pallas kernels  170 us (39%)
  starting transfers between devices  45.5 us (10%)
  other arithmetic  9.99 us (2%)
  local copies, waits for them, and re-layouts  6.88 us (2%)
    ppermute x21, waiting for transfers between devices, swapped(): return lax.ppermute(value, axes[0], [(0, 1), (1, 0)])  142 us
    pallas_call x5, Pallas kernels, gradients(): pl.pallas_call(functools.partial(grads_body, embed_start is None), out_sh...  66 us
    pallas_call x2, Pallas kernels, later_pass(): pl.pallas_call(functools.partial(later_body, len(parts), tiles), out_shap...  46.8 us
    ppermute x7, waiting for transfers between devices, flipped(): lax.ppermute(value, axis, [(p, p ^ mask) for p in range(lax.axis_size(axi...  42 us
    pallas_call x1, Pallas kernels, first_pass(): pl.pallas_call(functools.partial(first_body, tiles), out_shape=shapes + [...  35.8 us
    ppermute x21, starting transfers between devices, swapped(): return lax.ppermute(value, axes[0], [(0, 1), (1, 0)])  19.8 us
    ppermute x18, starting transfers between devices, summands(): parts.append(lax.ppermute(parts[0], axes, pairs))  19 us
    pallas_call x5, Pallas kernels, placed_pieces(): pl.pallas_call(functools.partial(place_body, tiles, begin, tile), out_sha...  13 us
  transfers between devices with their start and end apart: 51, of which 17 were waited for; matrix products, arithmetic and copies ran while one was open for 2% of the time, Pallas kernels for 37%

profile of v2, /device:TPU:0, one launch (start us, length us, event | category | flops | bytes accessed | tf_op | source)
XLA Modules:
  0.0 435.0 jit_solution(8531812038818472742)
XLA Ops:
  2.0 2.5 collective-permute-start
  7.4 35.8 %first_pass.1 = (f32[1,1024]{1,0:T(1,128)}, f32[1,8192]{1,0:T(1,128)}, f32[1,8192]{1,0:T(1,128)}, f32[16,1024,1024]{2,1,0:T(8,128)}, bf16[512,1024]{1,0:T(8,128)...) custom-call(s32[4]{0:T(128)} %pad_add_fusion.places, f32[1]{0:T(128)} %bitcast.5.scale, ...), custom_call_target="tpu_custom_call" | custom-call | flops 17179869184 | bytes 83886080 | tf_op jit(solution)/shard_map/first_pass/pallas_call | solution.py:224
  50.9 2.6 collective-permute-start.8
  54.4 3.2 columns_of.3
  59.5 23.4 %later_pass.2 = (f32[1,1024]{1,0:T(1,128)}, f32[1,8192]{1,0:T(1,128)}, f32[1,8192]{1,0:T(1,128)}) custom-call(s32[4]{0:T(128)} %pad_add_fusion.places, f32[16,1024,1024]{2,1,0:T(8,128)} %get-tuple-element.48.powers, f32[1,1024]{1,0:T(1,128)} %copy-done.20, f32[1,1024]{1,0:T(1,128)} %copy-done.23, f32[1,1024]{1,0:T(1,128)} %copy-done.24, f32[1,1024]{1,0:T(1,128)} %copy-done.25), custom_call_target="tpu_custom_call" | custom-call | flops 67108864 | bytes 67108864 | tf_op jit(solution)/shard_map/later_pass/pallas_call | solution.py:256
  86.0 10.3 %collective-permute-done.10 = bf16[256,512]{1,0:T(8,128)(2,1)S(1)} collective-permute-done((bf16[256,512]{1,0:T(8,128)(2,1)S(1)}, bf16[256,512]{1,0:T(8,128)(2,1)S(1)}, u32[]{:S(2)}, u32[]{:S(2)}) %collective-permute-start.10) | collective-permute-done | bytes 262176 | tf_op jit(solution)/shard_map/ppermute | solution.py:479
  96.5 2.5 collective-permute-start.16
  99.0 1.9 collective-permute-start.17
  101.1 3.3 collective-permute-done.17.refs_3_
  105.0 23.4 %later_pass.3 = (f32[1,1024]{1,0:T(1,128)}, f32[1,8192]{1,0:T(1,128)}, f32[1,8192]{1,0:T(1,128)}) custom-call(s32[4]{0:T(128)} %pad_add_fusion.places, f32[16,1024,1024]{2,1,0:T(8,128)} %get-tuple-element.48.powers, f32[1,1024]{1,0:T(1,128)} %copy-done.21, f32[1,1024]{1,0:T(1,128)} %copy-done.26, f32[1,1024]{1,0:T(1,128)} %copy-done.27, f32[1,1024]{1,0:T(1,128)} %copy-done.28), custom_call_target="tpu_custom_call" | custom-call | flops 67108864 | bytes 67108864 | tf_op jit(solution)/shard_map/later_pass/pallas_call | solution.py:256
  130.4 2.0 collective-permute-done.20
  134.1 2.5 collective-permute-start.23
  136.5 1.9 collective-permute-start.24
  146.7 108.4 %collective-permute-done.25.refs_4_ = f32[1,1024]{1,0:T(1,128)S(1)} collective-permute-done((f32[1,1024]{1,0:T(1,128)S(1)}, f32[1,1024]{1,0:T(1,128)S(1)}, u32[]{:S(2)}, u32[]{:S(2)}) %collective-permute-start.25) | collective-permute-done | bytes 4128 | tf_op jit(solution)/shard_map/ppermute | solution.py:448
  260.4 2.8 final_scales.1
  264.2 10.0 %gradients.5 = (bf16[128,1024]{1,0:T(8,128)(2,1)}, bf16[128,1024]{1,0:T(8,128)(2,1)}, bf16[128,1024]{1,0:T(8,128)(2,1)}, bf16[128,1024]{1,0:T(8,128)(2,1)}, f32[1024,512]{1,0:T(8,128)}) custom-call(s32[4]{0:T(128)} %pad_add_fusion.places, bf16[1024,512]{1,0:T(8,128)(2,1)} %get-tuple-element.95.refs_8_.other_embed, ...), custom_call_target="tpu_custom_call" | custom-call | flops 3221225472 | bytes 11534336 | tf_op jit(solution)/shard_map/gradients/pallas_call | solution.py:367
  274.2 17.5 %gradients.6 = (bf16[128,2560]{1,0:T(8,128)(2,1)}, bf16[128,2560]{1,0:T(8,128)(2,1)}, bf16[128,2560]{1,0:T(8,128)(2,1)}, bf16[128,2560]{1,0:T(8,128)(2,1)}, f32[1024,512]{1,0:T(8,128)}) custom-call(s32[4]{0:T(128)} %pad_add_fusion.places, bf16[1024,512]{1,0:T(8,128)(2,1)} %get-tuple-element.95.refs_8_.other_embed, ...), custom_call_target="tpu_custom_call" | custom-call | flops 8053063680 | bytes 22544384 | tf_op jit(solution)/shard_map/gradients/pallas_call | solution.py:367
  291.7 15.2 %gradients.7 = (bf16[128,2048]{1,0:T(8,128)(2,1)}, bf16[128,2048]{1,0:T(8,128)(2,1)}, bf16[128,2048]{1,0:T(8,128)(2,1)}, bf16[128,2048]{1,0:T(8,128)(2,1)}, f32[1024,512]{1,0:T(8,128)}) custom-call(s32[4]{0:T(128)} %pad_add_fusion.places, bf16[1024,512]{1,0:T(8,128)(2,1)} %get-tuple-element.95.refs_8_.other_embed, ...), custom_call_target="tpu_custom_call" | custom-call | flops 6442450944 | bytes 18874368 | tf_op jit(solution)/shard_map/gradients/pallas_call | solution.py:367
  306.9 15.4 %gradients.8 = (bf16[128,2048]{1,0:T(8,128)(2,1)}, bf16[128,2048]{1,0:T(8,128)(2,1)}, bf16[128,2048]{1,0:T(8,128)(2,1)}, bf16[128,2048]{1,0:T(8,128)(2,1)}, f32[1024,512]{1,0:T(8,128)}) custom-call(s32[4]{0:T(128)} %pad_add_fusion.places, bf16[1024,512]{1,0:T(8,128)(2,1)} %get-tuple-element.95.refs_8_.other_embed, ...), custom_call_target="tpu_custom_call" | custom-call | flops 6442450944 | bytes 18874368 | tf_op jit(solution)/shard_map/gradients/pallas_call | solution.py:367
  323.1 8.0 %gradients.9 = (bf16[128,512]{1,0:T(8,128)(2,1)}, bf16[128,512]{1,0:T(8,128)(2,1)}, bf16[128,512]{1,0:T(8,128)(2,1)}, bf16[128,512]{1,0:T(8,128)(2,1)}, f32[1024,512]{1,0:T(8,128)}) custom-call(s32[4]{0:T(128)} %pad_add_fusion.places, bf16[1024,512]{1,0:T(8,128)(2,1)} %get-tuple-element.95.refs_8_.other_embed, ...), custom_call_target="tpu_custom_call" | custom-call | flops 1610612736 | bytes 7864320 | tf_op jit(solution)/shard_map/gradients/pallas_call | solution.py:367
  332.6 2.8 collective-permute-done.46
  339.7 11.3 %collective-permute-done.47 = f32[256,512]{1,0:T(8,128)S(1)} collective-permute-done((f32[256,512]{1,0:T(8,128)S(1)}, f32[256,512]{1,0:T(8,128)S(1)}, u32[]{:S(2)}, u32[]{:S(2)}) %collective-permute-start.47) | collective-permute-done | bytes 524320 | tf_op jit(solution)/shard_map/ppermute | solution.py:479
  353.7 7.9 %collective-permute-done.48 = f32[128,512]{1,0:T(8,128)S(1)} collective-permute-done((f32[128,512]{1,0:T(8,128)S(1)}, f32[128,512]{1,0:T(8,128)S(1)}, u32[]{:S(2)}, u32[]{:S(2)}) %collective-permute-start.48) | collective-permute-done | bytes 262176 | tf_op jit(solution)/shard_map/ppermute | solution.py:479
  363.3 2.7 collective-permute-done.38.refs_2_
  366.1 10.6 %collective-permute-done.39.refs_3_ = bf16[128,2048]{1,0:T(8,128)(2,1)} collective-permute-done((bf16[128,2048]{1,0:T(8,128)(2,1)}, bf16[128,2048]{1,0:T(8,128)(2,1)}, u32[]{:S(2)}, u32[]{:S(2)}) %collective-permute-start.39) | collective-permute-done | bytes 524320 | tf_op jit(solution)/shard_map/ppermute | solution.py:447
  377.0 8.9 %collective-permute-done.49 = f32[64,512]{1,0:T(8,128)S(1)} collective-permute-done((f32[64,512]{1,0:T(8,128)S(1)}, f32[64,512]{1,0:T(8,128)S(1)}, u32[]{:S(2)}, u32[]{:S(2)}) %collective-permute-start.49) | collective-permute-done | bytes 131104 | tf_op jit(solution)/shard_map/ppermute | solution.py:479
  387.2 29.5 %collective-permute-done.35.refs_2_ = bf16[128,2048]{1,0:T(8,128)(2,1)} collective-permute-done((bf16[128,2048]{1,0:T(8,128)(2,1)}, bf16[128,2048]{1,0:T(8,128)(2,1)}, u32[]{:S(2)}, u32[]{:S(2)}) %collective-permute-start.35) | collective-permute-done | bytes 524320 | tf_op jit(solution)/shard_map/ppermute | solution.py:448
  420.5 2.2 placed_pieces.5.refs_4_
  422.8 3.2 placed_pieces.6.refs_4_
  426.0 2.9 placed_pieces.7.refs_4_
  428.9 2.9 placed_pieces.8.refs_4_
  432.5 1.9 placed_pieces.9
  (181 shorter events, 54.5 us)
Async XLA Ops:
  2.0 41.1 %collective-permute-start = (bf16[64,512]{1,0:T(8,128)(2,1)S(1)}, bf16[64,512]{1,0:T(8,128)(2,1)S(1)}, u32[]{:S(2)}, u32[]{:S(2)}) collective-permute-start(bf16[64,512]{1,0:T(8,128)(2,1)S(1)} %dynamic-slice_bitcast_fusion.6), channel_id=1, source_target_pairs={{0,16},{16,0},{1,17},{17,1},{2,18},{18,2},{3,19},{19,3},{4,20},{20... | collective-permute-start | bytes 196616 | tf_op jit(solution)/shard_map/ppermute | solution.py:448
  47.5 35.4 %collective-permute-start.3 = (bf16[128,512]{1,0:T(8,128)(2,1)S(1)}, bf16[128,512]{1,0:T(8,128)(2,1)S(1)}, u32[]{:S(2)}, u32[]{:S(2)}) collective-permute-start(bf16[128,512]{1,0:T(8,128)(2,1)S(1)} %pad_maximum_fusion.5), channel_id=1, source_target_pairs={{0,4},{2,6},{4,0},{6,2},{8,12},{10,14},{12,8},{14,10},{1,5},{3,7},... | collective-permute-start | bytes 393224 | tf_op jit(solution)/shard_map/ppermute | solution.py:479
  57.6 216.6 %collective-permute-start.29 = (bf16[512,2560]{1,0:T(8,128)(2,1)}, bf16[512,2560]{1,0:T(8,128)(2,1)}, u32[]{:S(2)}, u32[]{:S(2)}) collective-permute-start(bf16[512,2560]{1,0:T(8,128)(2,1)} %columns_of.3), channel_id=1, source_target_pairs={{0,16},{16,0},{1,17},{17,1},{2,18},{18,2},{3,19},{19,3},{4,20},{20... | collective-permute-start | bytes 7864328 | tf_op jit(solution)/shard_map/ppermute | solution.py:448
  83.0 13.3 %collective-permute-start.10 = (bf16[256,512]{1,0:T(8,128)(2,1)S(1)}, bf16[256,512]{1,0:T(8,128)(2,1)S(1)}, u32[]{:S(2)}, u32[]{:S(2)}) collective-permute-start(bf16[256,512]{1,0:T(8,128)(2,1)S(1)} %pad_maximum_fusion.4), channel_id=1, source_target_pairs={{0,8},{2,10},{4,12},{6,14},{8,0},{10,2},{12,4},{14,6},{1,9},{3,11}... | collective-permute-start | bytes 786440 | tf_op jit(solution)/shard_map/ppermute | solution.py:479
  84.1 12.3 %collective-permute-start.12 = (f32[1,1024]{1,0:T(1,128)}, f32[1,1024]{1,0:T(1,128)S(1)}, u32[]{:S(2)}, u32[]{:S(2)}) collective-permute-start(f32[1,1024]{1,0:T(1,128)} %get-tuple-element.49), channel_id=1, source_target_pairs={{0,1},{1,0},{2,3},{3,2},{4,5},{5,4},{6,7},{7,6},{8,9},{9,8},{10,11... | collective-permute-start | bytes 12296 | tf_op jit(solution)/shard_map/ppermute | solution.py:464
  84.1 12.3 %collective-permute-start.13 = (f32[1,1024]{1,0:T(1,128)}, f32[1,1024]{1,0:T(1,128)S(1)}, u32[]{:S(2)}, u32[]{:S(2)}) collective-permute-start(f32[1,1024]{1,0:T(1,128)} %get-tuple-element.49), channel_id=1, source_target_pairs={{0,2},{1,3},{2,0},{3,1},{4,6},{5,7},{6,4},{7,5},{8,10},{9,11},{10,... | collective-permute-start | bytes 12296 | tf_op jit(solution)/shard_map/ppermute | solution.py:464
  85.6 10.8 %collective-permute-start.14 = (f32[1,1024]{1,0:T(1,128)}, f32[1,1024]{1,0:T(1,128)S(1)}, u32[]{:S(2)}, u32[]{:S(2)}) collective-permute-start(f32[1,1024]{1,0:T(1,128)} %get-tuple-element.49), channel_id=1, source_target_pairs={{0,3},{1,2},{2,1},{3,0},{4,7},{5,6},{6,5},{7,4},{8,11},{9,10},{10,... | collective-permute-start | bytes 12296 | tf_op jit(solution)/shard_map/ppermute | solution.py:464
  96.3 47.6 %collective-permute-start.11 = (bf16[512,512]{1,0:T(8,128)(2,1)S(1)}, bf16[512,512]{1,0:T(8,128)(2,1)S(1)}, u32[]{:S(2)}, u32[]{:S(2)}) collective-permute-start(bf16[512,512]{1,0:T(8,128)(2,1)S(1)} %pad_maximum_fusion.3), channel_id=1, source_target_pairs={{0,1},{1,0},{2,3},{3,2},{4,5},{5,4},{6,7},{7,6},{8,9},{9,8},{10,11... | collective-permute-start | bytes 1572872 | tf_op jit(solution)/shard_map/ppermute | solution.py:448
  140.4 122.8 %collective-permute-start.30 = (bf16[512,1024]{1,0:T(8,128)(2,1)}, bf16[512,1024]{1,0:T(8,128)(2,1)S(1)}, u32[]{:S(2)}, u32[]{:S(2)}) collective-permute-start(bf16[512,1024]{1,0:T(8,128)(2,1)} %get-tuple-element.62), channel_id=1, source_target_pairs={{0,16},{16,0},{1,17},{17,1},{2,18},{18,2},{3,19},{19,3},{4,20},{20... | collective-permute-start | bytes 3145736 | tf_op jit(solution)/shard_map/ppermute | solution.py:448
  141.9 149.9 %collective-permute-start.28 = (bf16[512,2048]{1,0:T(8,128)(2,1)}, bf16[512,2048]{1,0:T(8,128)(2,1)}, u32[]{:S(2)}, u32[]{:S(2)}) collective-permute-start(bf16[512,2048]{1,0:T(8,128)(2,1)} %get-tuple-element.61), channel_id=1, source_target_pairs={{0,16},{16,0},{1,17},{17,1},{2,18},{18,2},{3,19},{19,3},{4,20},{20... | collective-permute-start | bytes 6291464 | tf_op jit(solution)/shard_map/ppermute | solution.py:448
  142.5 164.5 %collective-permute-start.27 = (bf16[512,2048]{1,0:T(8,128)(2,1)}, bf16[512,2048]{1,0:T(8,128)(2,1)}, u32[]{:S(2)}, u32[]{:S(2)}) collective-permute-start(bf16[512,2048]{1,0:T(8,128)(2,1)} %get-tuple-element.60), channel_id=1, source_target_pairs={{0,16},{16,0},{1,17},{17,1},{2,18},{18,2},{3,19},{19,3},{4,20},{20... | collective-permute-start | bytes 6291464 | tf_op jit(solution)/shard_map/ppermute | solution.py:448
  143.9 111.1 %collective-permute-start.25 = (f32[1,1024]{1,0:T(1,128)S(1)}, f32[1,1024]{1,0:T(1,128)S(1)}, u32[]{:S(2)}, u32[]{:S(2)}) collective-permute-start(f32[1,1024]{1,0:T(1,128)S(1)} %add_divide_fusion), channel_id=1, source_target_pairs={{0,16},{16,0},{1,17},{17,1},{2,18},{18,2},{3,19},{19,3},{4,20},{20... | collective-permute-start | bytes 12296 | tf_op jit(solution)/shard_map/ppermute | solution.py:448
  259.0 63.3 %collective-permute-start.18 = (bf16[512,512]{1,0:T(8,128)(2,1)}, bf16[512,512]{1,0:T(8,128)(2,1)S(1)}, u32[]{:S(2)}, u32[]{:S(2)}) collective-permute-start(bf16[512,512]{1,0:T(8,128)(2,1)} %columns_of.2), channel_id=1, source_target_pairs={{0,16},{16,0},{1,17},{17,1},{2,18},{18,2},{3,19},{19,3},{4,20},{20... | collective-permute-start | bytes 1572872 | tf_op jit(solution)/shard_map/ppermute | solution.py:448
  336.9 14.0 %collective-permute-start.47 = (f32[256,512]{1,0:T(8,128)S(1)}, f32[256,512]{1,0:T(8,128)S(1)}, u32[]{:S(2)}, u32[]{:S(2)}) collective-permute-start(f32[256,512]{1,0:T(8,128)S(1)} %bitcast.69), channel_id=1, source_target_pairs={{0,2},{2,0},{4,6},{6,4},{8,10},{10,8},{12,14},{14,12},{1,3},{3,1},... | collective-permute-start | bytes 1572872 | tf_op jit(solution)/shard_map/ppermute | solution.py:479
  337.5 15.3 %collective-permute-start.43 = (bf16[128,1024]{1,0:T(8,128)(2,1)S(1)}, bf16[128,1024]{1,0:T(8,128)(2,1)S(1)}, u32[]{:S(2)}, u32[]{:S(2)}) collective-permute-start(bf16[128,1024]{1,0:T(8,128)(2,1)S(1)} %copy-done.30), channel_id=1, source_target_pairs={{0,1},{1,0},{2,3},{3,2},{4,5},{5,4},{6,7},{7,6},{8,9},{9,8},{10,11... | collective-permute-start | bytes 786440 | tf_op jit(solution)/shard_map/ppermute | solution.py:448
  337.5 15.5 %collective-permute-start.44 = (bf16[128,1024]{1,0:T(8,128)(2,1)}, bf16[128,1024]{1,0:T(8,128)(2,1)S(1)}, u32[]{:S(2)}, u32[]{:S(2)}) collective-permute-start(bf16[128,1024]{1,0:T(8,128)(2,1)} %get-tuple-element.85), channel_id=1, source_target_pairs={{0,16},{16,0},{1,17},{17,1},{2,18},{18,2},{3,19},{19,3},{4,20},{20... | collective-permute-start | bytes 786440 | tf_op jit(solution)/shard_map/ppermute | solution.py:448
  339.3 13.8 %collective-permute-start.45 = (bf16[128,1024]{1,0:T(8,128)(2,1)}, bf16[128,1024]{1,0:T(8,128)(2,1)S(1)}, u32[]{:S(2)}, u32[]{:S(2)}) collective-permute-start(bf16[128,1024]{1,0:T(8,128)(2,1)} %get-tuple-element.86), channel_id=1, source_target_pairs={{0,17},{1,16},{16,1},{17,0},{2,19},{3,18},{18,3},{19,2},{4,21},{5,... | collective-permute-start | bytes 786440 | tf_op jit(solution)/shard_map/ppermute | solution.py:447
  339.4 14.1 %collective-permute-start.37 = (bf16[128,2048]{1,0:T(8,128)(2,1)}, bf16[128,2048]{1,0:T(8,128)(2,1)S(1)}, u32[]{:S(2)}, u32[]{:S(2)}) collective-permute-start(bf16[128,2048]{1,0:T(8,128)(2,1)} %get-tuple-element.76), channel_id=1, source_target_pairs={{0,1},{1,0},{2,3},{3,2},{4,5},{5,4},{6,7},{7,6},{8,9},{9,8},{10,11... | collective-permute-start | bytes 1572872 | tf_op jit(solution)/shard_map/ppermute | solution.py:448
  351.0 15.0 %collective-permute-start.38 = (bf16[128,2048]{1,0:T(8,128)(2,1)}, bf16[128,2048]{1,0:T(8,128)(2,1)S(1)}, u32[]{:S(2)}, u32[]{:S(2)}) collective-permute-start(bf16[128,2048]{1,0:T(8,128)(2,1)} %get-tuple-element.77), channel_id=1, source_target_pairs={{0,16},{16,0},{1,17},{17,1},{2,18},{18,2},{3,19},{19,3},{4,20},{20... | collective-permute-start | bytes 1572872 | tf_op jit(solution)/shard_map/ppermute | solution.py:448
  352.9 23.8 %collective-permute-start.39 = (bf16[128,2048]{1,0:T(8,128)(2,1)}, bf16[128,2048]{1,0:T(8,128)(2,1)}, u32[]{:S(2)}, u32[]{:S(2)}) collective-permute-start(bf16[128,2048]{1,0:T(8,128)(2,1)} %get-tuple-element.78), channel_id=1, source_target_pairs={{0,17},{1,16},{16,1},{17,0},{2,19},{3,18},{18,3},{19,2},{4,21},{5,... | collective-permute-start | bytes 1572872 | tf_op jit(solution)/shard_map/ppermute | solution.py:447
  353.0 8.6 %collective-permute-start.48 = (f32[128,512]{1,0:T(8,128)S(1)}, f32[128,512]{1,0:T(8,128)S(1)}, u32[]{:S(2)}, u32[]{:S(2)}) collective-permute-start(f32[128,512]{1,0:T(8,128)S(1)} %bitcast.70), channel_id=1, source_target_pairs={{0,4},{2,6},{4,0},{6,2},{8,12},{10,14},{12,8},{14,10},{1,5},{3,7},... | collective-permute-start | bytes 786440 | tf_op jit(solution)/shard_map/ppermute | solution.py:479
  353.1 23.8 %collective-permute-start.34 = (bf16[128,2048]{1,0:T(8,128)(2,1)}, bf16[128,2048]{1,0:T(8,128)(2,1)}, u32[]{:S(2)}, u32[]{:S(2)}) collective-permute-start(bf16[128,2048]{1,0:T(8,128)(2,1)} %get-tuple-element.72), channel_id=1, source_target_pairs={{0,1},{1,0},{2,3},{3,2},{4,5},{5,4},{6,7},{7,6},{8,9},{9,8},{10,11... | collective-permute-start | bytes 1572872 | tf_op jit(solution)/shard_map/ppermute | solution.py:448
  353.5 63.1 %collective-permute-start.40 = (bf16[128,2560]{1,0:T(8,128)(2,1)}, bf16[128,2560]{1,0:T(8,128)(2,1)S(1)}, u32[]{:S(2)}, u32[]{:S(2)}) collective-permute-start(bf16[128,2560]{1,0:T(8,128)(2,1)} %get-tuple-element.80), channel_id=1, source_target_pairs={{0,1},{1,0},{2,3},{3,2},{4,5},{5,4},{6,7},{7,6},{8,9},{9,8},{10,11... | collective-permute-start | bytes 1966088 | tf_op jit(solution)/shard_map/ppermute | solution.py:448
  361.6 56.9 %collective-permute-start.41 = (bf16[128,2560]{1,0:T(8,128)(2,1)}, bf16[128,2560]{1,0:T(8,128)(2,1)S(1)}, u32[]{:S(2)}, u32[]{:S(2)}) collective-permute-start(bf16[128,2560]{1,0:T(8,128)(2,1)} %get-tuple-element.81), channel_id=1, source_target_pairs={{0,16},{16,0},{1,17},{17,1},{2,18},{18,2},{3,19},{19,3},{4,20},{20... | collective-permute-start | bytes 1966088 | tf_op jit(solution)/shard_map/ppermute | solution.py:448
  366.0 52.8 %collective-permute-start.42 = (bf16[128,2560]{1,0:T(8,128)(2,1)}, bf16[128,2560]{1,0:T(8,128)(2,1)S(1)}, u32[]{:S(2)}, u32[]{:S(2)}) collective-permute-start(bf16[128,2560]{1,0:T(8,128)(2,1)} %get-tuple-element.82), channel_id=1, source_target_pairs={{0,17},{1,16},{16,1},{17,0},{2,19},{3,18},{18,3},{19,2},{4,21},{5,... | collective-permute-start | bytes 1966088 | tf_op jit(solution)/shard_map/ppermute | solution.py:447
  376.6 40.0 %collective-permute-start.35 = (bf16[128,2048]{1,0:T(8,128)(2,1)}, bf16[128,2048]{1,0:T(8,128)(2,1)}, u32[]{:S(2)}, u32[]{:S(2)}) collective-permute-start(bf16[128,2048]{1,0:T(8,128)(2,1)} %get-tuple-element.73), channel_id=1, source_target_pairs={{0,16},{16,0},{1,17},{17,1},{2,18},{18,2},{3,19},{19,3},{4,20},{20... | collective-permute-start | bytes 1572872 | tf_op jit(solution)/shard_map/ppermute | solution.py:448
  376.9 8.9 %collective-permute-start.49 = (f32[64,512]{1,0:T(8,128)S(1)}, f32[64,512]{1,0:T(8,128)S(1)}, u32[]{:S(2)}, u32[]{:S(2)}) collective-permute-start(f32[64,512]{1,0:T(8,128)S(1)} %dynamic-slice_bitcast_fusion.5), channel_id=1, source_target_pairs={{0,8},{2,10},{4,12},{6,14},{8,0},{10,2},{12,4},{14,6},{1,9},{3,11}... | collective-permute-start | bytes 393224 | tf_op jit(solution)/shard_map/ppermute | solution.py:479
  385.8 43.0 %collective-permute-start.36 = (bf16[128,2048]{1,0:T(8,128)(2,1)}, bf16[128,2048]{1,0:T(8,128)(2,1)}, u32[]{:S(2)}, u32[]{:S(2)}) collective-permute-start(bf16[128,2048]{1,0:T(8,128)(2,1)} %get-tuple-element.74), channel_id=1, source_target_pairs={{0,17},{1,16},{16,1},{17,0},{2,19},{3,18},{18,3},{19,2},{4,21},{5,... | collective-permute-start | bytes 1572872 | tf_op jit(solution)/shard_map/ppermute | solution.py:447
  416.6 15.1 %collective-permute-start.31 = (bf16[128,512]{1,0:T(8,128)(2,1)}, bf16[128,512]{1,0:T(8,128)(2,1)S(1)}, u32[]{:S(2)}, u32[]{:S(2)}) collective-permute-start(bf16[128,512]{1,0:T(8,128)(2,1)} %get-tuple-element.68), channel_id=1, source_target_pairs={{0,1},{1,0},{2,3},{3,2},{4,5},{5,4},{6,7},{7,6},{8,9},{9,8},{10,11... | collective-permute-start | bytes 393224 | tf_op jit(solution)/shard_map/ppermute | solution.py:448
  416.7 15.1 %collective-permute-start.32 = (bf16[128,512]{1,0:T(8,128)(2,1)}, bf16[128,512]{1,0:T(8,128)(2,1)S(1)}, u32[]{:S(2)}, u32[]{:S(2)}) collective-permute-start(bf16[128,512]{1,0:T(8,128)(2,1)} %get-tuple-element.69), channel_id=1, source_target_pairs={{0,16},{16,0},{1,17},{17,1},{2,18},{18,2},{3,19},{19,3},{4,20},{20... | collective-permute-start | bytes 393224 | tf_op jit(solution)/shard_map/ppermute | solution.py:448
  418.5 13.3 %collective-permute-start.33 = (bf16[128,512]{1,0:T(8,128)(2,1)}, bf16[128,512]{1,0:T(8,128)(2,1)}, u32[]{:S(2)}, u32[]{:S(2)}) collective-permute-start(bf16[128,512]{1,0:T(8,128)(2,1)} %get-tuple-element.70), channel_id=1, source_target_pairs={{0,17},{1,16},{16,1},{17,0},{2,19},{3,18},{18,3},{19,2},{4,21},{5,... | collective-permute-start | bytes 393224 | tf_op jit(solution)/shard_map/ppermute | solution.py:447
  418.8 15.6 %collective-permute-start.50 = (f32[64,256]{1,0:T(8,128)S(1)}, f32[64,256]{1,0:T(8,128)S(1)}, u32[]{:S(2)}, u32[]{:S(2)}) collective-permute-start(f32[64,256]{1,0:T(8,128)S(1)} %bitcast.71), channel_id=1, source_target_pairs={{0,16},{16,0},{1,17},{17,1},{2,18},{18,2},{3,19},{19,3},{4,20},{20... | collective-permute-start | bytes 196616 | tf_op jit(solution)/shard_map/ppermute | solution.py:448
  (51 other events, 460.3 us)

commit v3 on v2

--- a/solution.py
+++ b/solution.py
@@ -2,6 +2,7 @@
 
 import jax
 import jax.numpy as jnp
+import numpy as np
 from jax import lax
 from jax.experimental import pallas as pl
 from jax.experimental.pallas import tpu as pltpu
@@ -9,7 +10,8 @@
 
 
 ITERS = 3
-LOG2E = 1.4426950408889634
+SHARPEN = float(np.float32(1) / np.float32(0.07))
+SOFTEN = float(np.float32(1) / np.float32(0.1))
 SHARES = (1, 5, 2, 4, 4)
 CHUNKS = len(SHARES)
 SLICED = 2
@@ -86,11 +88,15 @@
     )(matrix)
 
 
-def reciprocal_rows(parts, crops):
+def total_of(parts):
     total = parts[0][...]
     for part in parts[1:]:
         total = total + part[...]
-    return jnp.transpose(jnp.broadcast_to(1.0 / total, (128, crops)))
+    return total
+
+
+def as_rows(line):
+    return jnp.transpose(jnp.broadcast_to(line, (128, line.shape[1])))
 
 
 def folded(value):
@@ -101,18 +107,17 @@
 
 
 def finish_tile(places, tiles, step, total, powers, own_factor, partner_factor, sums):
-    factor = jnp.where(
-        places[0] == 1, 1.0, 1.0 / jnp.sum(total, axis=0, keepdims=True)
-    )
+    column_sum = jnp.where(places[0] == 1, 1.0, jnp.sum(total, axis=0, keepdims=True))
+    factor = 1.0 / column_sum
     owned = step // tiles == places[0]
 
     @pl.when(owned)
     def _():
-        own_factor[...] = factor
+        own_factor[...] = column_sum
 
     @pl.when(jnp.logical_not(owned))
     def _():
-        partner_factor[...] = factor
+        partner_factor[...] = column_sum
 
     for start in range(0, powers.shape[0], LINES):
         rows = pl.ds(start, LINES)
@@ -132,8 +137,8 @@
 
 
 def first_body(tiles, places, scale, embed, weight, *refs):
-    row_sums, own_factor, partner_factor, powers = refs[:4]
-    sent, sums = refs[4:-1], refs[-1]
+    row_sums, own_factor, partner_factor, logits = refs[:4]
+    sent, sums, powers = refs[4:-2], refs[-2], refs[-1]
     step = pl.program_id(0)
     crops = embed.shape[0]
     width = weight.shape[1]
@@ -147,7 +152,9 @@
     for start in range(0, crops, ROWS):
         rows = pl.ds(start, ROWS)
         scores = jnp.dot(embed[rows, :], block, preferred_element_type=jnp.float32)
-        part = jnp.exp2(scores * scale[0])
+        scaled = scores * scale[0]
+        logits[rows, :] = scaled
+        part = jnp.exp(scaled)
         powers[rows, :] = part
         total += jnp.sum(part.reshape(ROWS // 8, 8, width), axis=0)
     foreign = step // tiles != places[0]
@@ -162,29 +169,31 @@
     finish_pass(row_sums, sums)
 
 
-def later_body(nparts, tiles, places, powers, *refs):
+def later_body(nparts, tiles, places, logits, *refs):
     parts, refs = refs[:nparts], refs[nparts:]
-    row_sums, own_factor, partner_factor, sums, row_scale = refs
-    group, crops, width = powers.shape
+    row_sums, own_factor, partner_factor, sums, row_scale, powers = refs
+    group, crops, width = logits.shape
 
     @pl.when(pl.program_id(0) == 0)
     def _():
         sums[...] = jnp.zeros_like(sums)
-        row_scale[...] = reciprocal_rows(parts, crops)
+        row_scale[...] = as_rows(1.0 / total_of(parts))
 
     for place in range(group):
-        tile = powers.at[place]
+        tile = logits.at[place]
         lanes = pl.ds(place * width, width)
         total = jnp.zeros((8, width), jnp.float32)
         for start in range(0, crops, 8):
             rows = pl.ds(start, 8)
-            total += tile[rows, :] * lane_tiles(row_scale[rows, :], width)
+            part = jnp.exp(tile[rows, :])
+            powers[rows, :] = part
+            total += part * lane_tiles(row_scale[rows, :], width)
         finish_tile(
             places,
             tiles,
             pl.program_id(0) * group,
             total,
-            tile,
+            powers,
             own_factor.at[:, lanes],
             partner_factor.at[:, lanes],
             sums,
@@ -237,7 +246,10 @@
             out_specs=specs
             + [pl.BlockSpec((None, crops, tile), lambda t, places: (t, 0, 0))]
             + [sent_spec(begin, count) for begin, count in sent],
-            scratch_shapes=[pltpu.VMEM((crops, 128), jnp.float32)],
+            scratch_shapes=[
+                pltpu.VMEM((crops, 128), jnp.float32),
+                pltpu.VMEM((crops, tile), jnp.float32),
+            ],
         ),
         cost_estimate=cost(
             4 * crops * depth * quarter_width,
@@ -267,6 +279,7 @@
             scratch_shapes=[
                 pltpu.VMEM((crops, 128), jnp.float32),
                 pltpu.VMEM((crops, 128), jnp.float32),
+                pltpu.VMEM((crops, tile), jnp.float32),
             ],
         ),
         cost_estimate=cost(8 * crops * quarter_width, 8 * crops * quarter_width, 0),
@@ -275,15 +288,13 @@
 
 
 def scales_body(nparts, places, *refs):
-    parts, (got_inverse, own_factor, got_factor) = refs[:nparts], refs[nparts : nparts + 3]
-    row_scale, inverse_sum, column_scale = refs[-3:]
-    crops = got_inverse.shape[1]
-    mine = reciprocal_rows(parts, crops)
-    theirs = jnp.transpose(jnp.broadcast_to(got_inverse[...], (128, crops)))
+    parts, (got_total, own_sum, got_sum) = refs[:nparts], refs[nparts : nparts + 3]
+    row_shift, inverse_sum, column_shift = refs[-3:]
     teaches = places[0] == 0
-    row_scale[...] = jnp.where(teaches, mine, theirs)
-    inverse_sum[...] = jnp.where(teaches, theirs, mine)
-    column_scale[...] = jnp.where(teaches, own_factor[...], got_factor[...])
+    mine, theirs = total_of(parts), got_total[...]
+    row_shift[...] = as_rows(-jnp.log(jnp.where(teaches, mine, theirs)))
+    inverse_sum[...] = as_rows(1.0 / jnp.where(teaches, theirs, mine))
+    column_shift[...] = -jnp.log(jnp.where(teaches, own_sum[...], got_sum[...]))
 
 
 def final_scales(places, parts, got_inverse, own_factor, got_factor, ahead):
@@ -315,20 +326,20 @@
     def _():
         embed_total[...] = jnp.zeros_like(embed_total) if first else embed_start[...]
 
-    def tile(student, divisor, teaches):
+    def tile(student, sharpening, teaches):
         block = arrived[...]
         student_block = student[...]
-        factor = column_scale[...]
+        shift = column_scale[...]
         for start in range(0, crops, ROWS):
             rows = pl.ds(start, ROWS)
             scores = jnp.dot(other_embed[rows, :], block, preferred_element_type=jnp.float32)
-            computed = jnp.exp2(scores * (LOG2E / divisor))
+            computed = scores * sharpening
             read = powers[rows, :]
-            teacher, student_powers = (read, computed) if teaches else (computed, read)
-            targets = (teacher * factor * lane_tiles(row_scale[rows, :], width)).astype(
-                jnp.bfloat16
-            )
-            probs = student_powers * lane_tiles(inverse_sum[rows, :], width)
+            teacher, student_logits = (read, computed) if teaches else (computed, read)
+            targets = jnp.exp(
+                teacher + shift + lane_tiles(row_scale[rows, :], width)
+            ).astype(jnp.bfloat16)
+            probs = jnp.exp(student_logits) * lane_tiles(inverse_sum[rows, :], width)
             grads = ((probs - targets.astype(jnp.float32)) * 10.0).astype(jnp.bfloat16)
             logit_grads[rows, :] = grads
             embed_total[rows, :] += lax.dot_general(
@@ -343,11 +354,11 @@
 
     @pl.when(places[0] == 0)
     def _():
-        tile(arrived, 0.1, True)
+        tile(arrived, SOFTEN, True)
 
     @pl.when(places[0] == 1)
     def _():
-        tile(own, 0.07, False)
+        tile(own, SHARPEN, False)
 
 
 def gradients(
@@ -535,7 +546,7 @@
     role_embed = swapped(lax.dynamic_slice_in_dim(own_embed, part_start, part_rows), "role")
     own_all = joined(own_embed, crop_embed, crop_place)
 
-    scale = jnp.where(teaches, LOG2E / 0.07, LOG2E / 0.1).astype(jnp.float32).reshape(1)
+    scale = jnp.where(teaches, SHARPEN, SOFTEN).astype(jnp.float32).reshape(1)
     parts = []
     diagonal_embed = None
     for iteration in range(ITERS):
@@ -568,8 +579,7 @@
     )
 
     got_factor = swapped(partner_factor, "role")
-    inverse = 1.0 / functools.reduce(jnp.add, parts)
-    got_inverse = swapped(inverse, "role")
+    got_inverse = swapped(functools.reduce(jnp.add, parts), "role")
     row_scale, inverse_sum, columns = final_scales(
         places, parts, got_inverse, own_factor, got_factor, (turned, other_all)
     )

time: 437 us -> 443 us (1.014)
  Pallas kernels: 170 us -> 177 us
  transfers between devices with their start and end apart: 51 -> 51, of which waited for: 17 -> 17; matrix products, arithmetic and copies ran while one was open for 2% -> 2% of each run, Pallas kernels for 37% -> 38%
where the time goes in v3:
time: 443 us; the launch traced here: 442 us
  waiting for transfers between devices  201 us (45%)
  Pallas kernels  177 us (40%)
  starting transfers between devices  45.4 us (10%)
  other arithmetic  9.99 us (2%)
  local copies, waits for them, and re-layouts  6.88 us (2%)
    ppermute x21, waiting for transfers between devices, swapped(): return lax.ppermute(value, axes[0], [(0, 1), (1, 0)])  142 us
    pallas_call x5, Pallas kernels, gradients(): pl.pallas_call(functools.partial(grads_body, embed_start is None), out_sh...  69.1 us
    pallas_call x2, Pallas kernels, later_pass(): pl.pallas_call(functools.partial(later_body, len(parts), tiles), out_shap...  51.1 us
    ppermute x7, waiting for transfers between devices, flipped(): lax.ppermute(value, axis, [(p, p ^ mask) for p in range(lax.axis_size(axi...  41.8 us
    pallas_call x1, Pallas kernels, first_pass(): pl.pallas_call(functools.partial(first_body, tiles), out_shape=shapes + [...  36 us
    ppermute x18, starting transfers between devices, summands(): parts.append(lax.ppermute(parts[0], axes, pairs))  19 us
    ppermute x21, starting transfers between devices, swapped(): return lax.ppermute(value, axes[0], [(0, 1), (1, 0)])  18.7 us
    pallas_call x5, Pallas kernels, placed_pieces(): pl.pallas_call(functools.partial(place_body, tiles, begin, tile), out_sha...  13 us
  transfers between devices with their start and end apart: 51, of which 17 were waited for; matrix products, arithmetic and copies ran while one was open for 2% of the time, Pallas kernels for 38%

profile of v3, /device:TPU:0, one launch (start us, length us, event | category | flops | bytes accessed | tf_op | source)
XLA Modules:
  0.0 441.5 jit_solution(1295578134495275262)
XLA Ops:
  2.0 2.5 collective-permute-start
  7.4 36.0 %first_pass.1 = (f32[1,1024]{1,0:T(1,128)}, f32[1,8192]{1,0:T(1,128)}, f32[1,8192]{1,0:T(1,128)}, f32[16,1024,1024]{2,1,0:T(8,128)}, bf16[512,1024]{1,0:T(8,128)...) custom-call(s32[4]{0:T(128)} %pad_add_fusion.places, f32[1]{0:T(128)} %bitcast.5.scale, ...), custom_call_target="tpu_custom_call" | custom-call | flops 17179869184 | bytes 83886080 | tf_op jit(solution)/shard_map/first_pass/pallas_call | solution.py:233
  51.1 2.6 collective-permute-start.8
  54.5 3.2 columns_of.3
  59.7 25.6 %later_pass.2 = (f32[1,1024]{1,0:T(1,128)}, f32[1,8192]{1,0:T(1,128)}, f32[1,8192]{1,0:T(1,128)}) custom-call(s32[4]{0:T(128)} %pad_add_fusion.places, f32[16,1024,1024]{2,1,0:T(8,128)} %get-tuple-element.48.logits.powers, f32[1,1024]{1,0:T(1,128)} %copy-done.20, f32[1,1024]{1,0:T(1,128)} %copy-done.23, f32[1,1024]{1,0:T(1,128)} %copy-done.24, ...), custom_call_target="tpu_custom_call" | custom-call | flops 67108864 | bytes 67108864 | tf_op jit(solution)/shard_map/later_pass/pallas_call | solution.py:268
  88.3 10.2 %collective-permute-done.10 = bf16[256,512]{1,0:T(8,128)(2,1)S(1)} collective-permute-done((bf16[256,512]{1,0:T(8,128)(2,1)S(1)}, bf16[256,512]{1,0:T(8,128)(2,1)S(1)}, u32[]{:S(2)}, u32[]{:S(2)}) %collective-permute-start.10) | collective-permute-done | bytes 262176 | tf_op jit(solution)/shard_map/ppermute | solution.py:490
  98.9 2.5 collective-permute-start.16
  101.4 1.9 collective-permute-start.17
  103.5 3.3 collective-permute-done.17.refs_3_
  107.4 25.6 %later_pass.3 = (f32[1,1024]{1,0:T(1,128)}, f32[1,8192]{1,0:T(1,128)}, f32[1,8192]{1,0:T(1,128)}) custom-call(s32[4]{0:T(128)} %pad_add_fusion.places, f32[16,1024,1024]{2,1,0:T(8,128)} %get-tuple-element.48.logits.powers, f32[1,1024]{1,0:T(1,128)} %copy-done.21, f32[1,1024]{1,0:T(1,128)} %copy-done.26, f32[1,1024]{1,0:T(1,128)} %copy-done.27, ...), custom_call_target="tpu_custom_call" | custom-call | flops 67108864 | bytes 67108864 | tf_op jit(solution)/shard_map/later_pass/pallas_call | solution.py:268
  134.9 2.0 collective-permute-done.20
  138.6 2.4 collective-permute-start.23
  141.0 1.9 collective-permute-start.24
  151.2 108.4 %collective-permute-done.25.refs_4_ = f32[1,1024]{1,0:T(1,128)S(1)} collective-permute-done((f32[1,1024]{1,0:T(1,128)S(1)}, f32[1,1024]{1,0:T(1,128)S(1)}, u32[]{:S(2)}, u32[]{:S(2)}) %collective-permute-start.25) | collective-permute-done | bytes 4128 | tf_op jit(solution)/shard_map/ppermute | solution.py:459
  264.9 2.7 final_scales.1
  268.6 10.4 %gradients.5 = (bf16[128,1024]{1,0:T(8,128)(2,1)}, bf16[128,1024]{1,0:T(8,128)(2,1)}, bf16[128,1024]{1,0:T(8,128)(2,1)}, bf16[128,1024]{1,0:T(8,128)(2,1)}, f32[1024,512]{1,0:T(8,128)}) custom-call(s32[4]{0:T(128)} %pad_add_fusion.places, bf16[1024,512]{1,0:T(8,128)(2,1)} %get-tuple-element.95.refs_8_.other_embed, ...), custom_call_target="tpu_custom_call" | custom-call | flops 3221225472 | bytes 11534336 | tf_op jit(solution)/shard_map/gradients/pallas_call | solution.py:378
  278.9 18.3 %gradients.6 = (bf16[128,2560]{1,0:T(8,128)(2,1)}, bf16[128,2560]{1,0:T(8,128)(2,1)}, bf16[128,2560]{1,0:T(8,128)(2,1)}, bf16[128,2560]{1,0:T(8,128)(2,1)}, f32[1024,512]{1,0:T(8,128)}) custom-call(s32[4]{0:T(128)} %pad_add_fusion.places, bf16[1024,512]{1,0:T(8,128)(2,1)} %get-tuple-element.95.refs_8_.other_embed, ...), custom_call_target="tpu_custom_call" | custom-call | flops 8053063680 | bytes 22544384 | tf_op jit(solution)/shard_map/gradients/pallas_call | solution.py:378
  297.3 16.1 %gradients.7 = (bf16[128,2048]{1,0:T(8,128)(2,1)}, bf16[128,2048]{1,0:T(8,128)(2,1)}, bf16[128,2048]{1,0:T(8,128)(2,1)}, bf16[128,2048]{1,0:T(8,128)(2,1)}, f32[1024,512]{1,0:T(8,128)}) custom-call(s32[4]{0:T(128)} %pad_add_fusion.places, bf16[1024,512]{1,0:T(8,128)(2,1)} %get-tuple-element.95.refs_8_.other_embed, ...), custom_call_target="tpu_custom_call" | custom-call | flops 6442450944 | bytes 18874368 | tf_op jit(solution)/shard_map/gradients/pallas_call | solution.py:378
  313.4 15.9 %gradients.8 = (bf16[128,2048]{1,0:T(8,128)(2,1)}, bf16[128,2048]{1,0:T(8,128)(2,1)}, bf16[128,2048]{1,0:T(8,128)(2,1)}, bf16[128,2048]{1,0:T(8,128)(2,1)}, f32[1024,512]{1,0:T(8,128)}) custom-call(s32[4]{0:T(128)} %pad_add_fusion.places, bf16[1024,512]{1,0:T(8,128)(2,1)} %get-tuple-element.95.refs_8_.other_embed, ...), custom_call_target="tpu_custom_call" | custom-call | flops 6442450944 | bytes 18874368 | tf_op jit(solution)/shard_map/gradients/pallas_call | solution.py:378
  330.1 8.4 %gradients.9 = (bf16[128,512]{1,0:T(8,128)(2,1)}, bf16[128,512]{1,0:T(8,128)(2,1)}, bf16[128,512]{1,0:T(8,128)(2,1)}, bf16[128,512]{1,0:T(8,128)(2,1)}, f32[1024,512]{1,0:T(8,128)}) custom-call(s32[4]{0:T(128)} %pad_add_fusion.places, bf16[1024,512]{1,0:T(8,128)(2,1)} %get-tuple-element.95.refs_8_.other_embed, ...), custom_call_target="tpu_custom_call" | custom-call | flops 1610612736 | bytes 7864320 | tf_op jit(solution)/shard_map/gradients/pallas_call | solution.py:378
  340.0 2.8 collective-permute-done.46
  347.1 11.3 %collective-permute-done.47 = f32[256,512]{1,0:T(8,128)S(1)} collective-permute-done((f32[256,512]{1,0:T(8,128)S(1)}, f32[256,512]{1,0:T(8,128)S(1)}, u32[]{:S(2)}, u32[]{:S(2)}) %collective-permute-start.47) | collective-permute-done | bytes 524320 | tf_op jit(solution)/shard_map/ppermute | solution.py:490
  361.0 7.6 %collective-permute-done.48 = f32[128,512]{1,0:T(8,128)S(1)} collective-permute-done((f32[128,512]{1,0:T(8,128)S(1)}, f32[128,512]{1,0:T(8,128)S(1)}, u32[]{:S(2)}, u32[]{:S(2)}) %collective-permute-start.48) | collective-permute-done | bytes 262176 | tf_op jit(solution)/shard_map/ppermute | solution.py:490
  370.9 2.5 collective-permute-done.38.refs_2_
  373.5 9.7 %collective-permute-done.39.refs_3_ = bf16[128,2048]{1,0:T(8,128)(2,1)} collective-permute-done((bf16[128,2048]{1,0:T(8,128)(2,1)}, bf16[128,2048]{1,0:T(8,128)(2,1)}, u32[]{:S(2)}, u32[]{:S(2)}) %collective-permute-start.39) | collective-permute-done | bytes 524320 | tf_op jit(solution)/shard_map/ppermute | solution.py:458
  384.4 9.0 %collective-permute-done.49 = f32[64,512]{1,0:T(8,128)S(1)} collective-permute-done((f32[64,512]{1,0:T(8,128)S(1)}, f32[64,512]{1,0:T(8,128)S(1)}, u32[]{:S(2)}, u32[]{:S(2)}) %collective-permute-start.49) | collective-permute-done | bytes 131104 | tf_op jit(solution)/shard_map/ppermute | solution.py:490
  394.1 29.9 %collective-permute-done.35.refs_2_ = bf16[128,2048]{1,0:T(8,128)(2,1)} collective-permute-done((bf16[128,2048]{1,0:T(8,128)(2,1)}, bf16[128,2048]{1,0:T(8,128)(2,1)}, u32[]{:S(2)}, u32[]{:S(2)}) %collective-permute-start.35) | collective-permute-done | bytes 524320 | tf_op jit(solution)/shard_map/ppermute | solution.py:459
  427.1 2.2 placed_pieces.5.refs_4_
  429.3 3.2 placed_pieces.6.refs_4_
  432.5 2.9 placed_pieces.7.refs_4_
  435.4 2.9 placed_pieces.8.refs_4_
  439.0 1.9 placed_pieces.9
  (181 shorter events, 54.5 us)
Async XLA Ops:
  2.0 41.3 %collective-permute-start = (bf16[64,512]{1,0:T(8,128)(2,1)S(1)}, bf16[64,512]{1,0:T(8,128)(2,1)S(1)}, u32[]{:S(2)}, u32[]{:S(2)}) collective-permute-start(bf16[64,512]{1,0:T(8,128)(2,1)S(1)} %dynamic-slice_bitcast_fusion.6), channel_id=1, source_target_pairs={{0,16},{16,0},{1,17},{17,1},{2,18},{18,2},{3,19},{19,3},{4,20},{20... | collective-permute-start | bytes 196616 | tf_op jit(solution)/shard_map/ppermute | solution.py:459
  47.7 37.5 %collective-permute-start.3 = (bf16[128,512]{1,0:T(8,128)(2,1)S(1)}, bf16[128,512]{1,0:T(8,128)(2,1)S(1)}, u32[]{:S(2)}, u32[]{:S(2)}) collective-permute-start(bf16[128,512]{1,0:T(8,128)(2,1)S(1)} %pad_maximum_fusion.5), channel_id=1, source_target_pairs={{0,4},{2,6},{4,0},{6,2},{8,12},{10,14},{12,8},{14,10},{1,5},{3,7},... | collective-permute-start | bytes 393224 | tf_op jit(solution)/shard_map/ppermute | solution.py:490
  57.8 221.1 %collective-permute-start.29 = (bf16[512,2560]{1,0:T(8,128)(2,1)}, bf16[512,2560]{1,0:T(8,128)(2,1)}, u32[]{:S(2)}, u32[]{:S(2)}) collective-permute-start(bf16[512,2560]{1,0:T(8,128)(2,1)} %columns_of.3), channel_id=1, source_target_pairs={{0,16},{16,0},{1,17},{17,1},{2,18},{18,2},{3,19},{19,3},{4,20},{20... | collective-permute-start | bytes 7864328 | tf_op jit(solution)/shard_map/ppermute | solution.py:459
  85.3 13.3 %collective-permute-start.10 = (bf16[256,512]{1,0:T(8,128)(2,1)S(1)}, bf16[256,512]{1,0:T(8,128)(2,1)S(1)}, u32[]{:S(2)}, u32[]{:S(2)}) collective-permute-start(bf16[256,512]{1,0:T(8,128)(2,1)S(1)} %pad_maximum_fusion.4), channel_id=1, source_target_pairs={{0,8},{2,10},{4,12},{6,14},{8,0},{10,2},{12,4},{14,6},{1,9},{3,11}... | collective-permute-start | bytes 786440 | tf_op jit(solution)/shard_map/ppermute | solution.py:490
  86.5 12.3 %collective-permute-start.12 = (f32[1,1024]{1,0:T(1,128)}, f32[1,1024]{1,0:T(1,128)S(1)}, u32[]{:S(2)}, u32[]{:S(2)}) collective-permute-start(f32[1,1024]{1,0:T(1,128)} %get-tuple-element.49), channel_id=1, source_target_pairs={{0,1},{1,0},{2,3},{3,2},{4,5},{5,4},{6,7},{7,6},{8,9},{9,8},{10,11... | collective-permute-start | bytes 12296 | tf_op jit(solution)/shard_map/ppermute | solution.py:475
  86.5 12.3 %collective-permute-start.13 = (f32[1,1024]{1,0:T(1,128)}, f32[1,1024]{1,0:T(1,128)S(1)}, u32[]{:S(2)}, u32[]{:S(2)}) collective-permute-start(f32[1,1024]{1,0:T(1,128)} %get-tuple-element.49), channel_id=1, source_target_pairs={{0,2},{1,3},{2,0},{3,1},{4,6},{5,7},{6,4},{7,5},{8,10},{9,11},{10,... | collective-permute-start | bytes 12296 | tf_op jit(solution)/shard_map/ppermute | solution.py:475
  88.0 10.8 %collective-permute-start.14 = (f32[1,1024]{1,0:T(1,128)}, f32[1,1024]{1,0:T(1,128)S(1)}, u32[]{:S(2)}, u32[]{:S(2)}) collective-permute-start(f32[1,1024]{1,0:T(1,128)} %get-tuple-element.49), channel_id=1, source_target_pairs={{0,3},{1,2},{2,1},{3,0},{4,7},{5,6},{6,5},{7,4},{8,11},{9,10},{10,... | collective-permute-start | bytes 12296 | tf_op jit(solution)/shard_map/ppermute | solution.py:475
  98.7 49.8 %collective-permute-start.11 = (bf16[512,512]{1,0:T(8,128)(2,1)S(1)}, bf16[512,512]{1,0:T(8,128)(2,1)S(1)}, u32[]{:S(2)}, u32[]{:S(2)}) collective-permute-start(bf16[512,512]{1,0:T(8,128)(2,1)S(1)} %pad_maximum_fusion.3), channel_id=1, source_target_pairs={{0,1},{1,0},{2,3},{3,2},{4,5},{5,4},{6,7},{7,6},{8,9},{9,8},{10,11... | collective-permute-start | bytes 1572872 | tf_op jit(solution)/shard_map/ppermute | solution.py:459
  144.9 122.7 %collective-permute-start.30 = (bf16[512,1024]{1,0:T(8,128)(2,1)}, bf16[512,1024]{1,0:T(8,128)(2,1)S(1)}, u32[]{:S(2)}, u32[]{:S(2)}) collective-permute-start(bf16[512,1024]{1,0:T(8,128)(2,1)} %get-tuple-element.62), channel_id=1, source_target_pairs={{0,16},{16,0},{1,17},{17,1},{2,18},{18,2},{3,19},{19,3},{4,20},{20... | collective-permute-start | bytes 3145736 | tf_op jit(solution)/shard_map/ppermute | solution.py:459
  146.4 150.9 %collective-permute-start.28 = (bf16[512,2048]{1,0:T(8,128)(2,1)}, bf16[512,2048]{1,0:T(8,128)(2,1)}, u32[]{:S(2)}, u32[]{:S(2)}) collective-permute-start(bf16[512,2048]{1,0:T(8,128)(2,1)} %get-tuple-element.61), channel_id=1, source_target_pairs={{0,16},{16,0},{1,17},{17,1},{2,18},{18,2},{3,19},{19,3},{4,20},{20... | collective-permute-start | bytes 6291464 | tf_op jit(solution)/shard_map/ppermute | solution.py:459
  147.0 166.4 %collective-permute-start.27 = (bf16[512,2048]{1,0:T(8,128)(2,1)}, bf16[512,2048]{1,0:T(8,128)(2,1)}, u32[]{:S(2)}, u32[]{:S(2)}) collective-permute-start(bf16[512,2048]{1,0:T(8,128)(2,1)} %get-tuple-element.60), channel_id=1, source_target_pairs={{0,16},{16,0},{1,17},{17,1},{2,18},{18,2},{3,19},{19,3},{4,20},{20... | collective-permute-start | bytes 6291464 | tf_op jit(solution)/shard_map/ppermute | solution.py:459
  148.4 111.1 %collective-permute-start.25 = (f32[1,1024]{1,0:T(1,128)S(1)}, f32[1,1024]{1,0:T(1,128)S(1)}, u32[]{:S(2)}, u32[]{:S(2)}) collective-permute-start(f32[1,1024]{1,0:T(1,128)S(1)} %add_add_fusion), channel_id=1, source_target_pairs={{0,16},{16,0},{1,17},{17,1},{2,18},{18,2},{3,19},{19,3},{4,20},{20... | collective-permute-start | bytes 12296 | tf_op jit(solution)/shard_map/ppermute | solution.py:459
  263.5 65.8 %collective-permute-start.18 = (bf16[512,512]{1,0:T(8,128)(2,1)}, bf16[512,512]{1,0:T(8,128)(2,1)S(1)}, u32[]{:S(2)}, u32[]{:S(2)}) collective-permute-start(bf16[512,512]{1,0:T(8,128)(2,1)} %columns_of.2), channel_id=1, source_target_pairs={{0,16},{16,0},{1,17},{17,1},{2,18},{18,2},{3,19},{19,3},{4,20},{20... | collective-permute-start | bytes 1572872 | tf_op jit(solution)/shard_map/ppermute | solution.py:459
  344.3 14.0 %collective-permute-start.47 = (f32[256,512]{1,0:T(8,128)S(1)}, f32[256,512]{1,0:T(8,128)S(1)}, u32[]{:S(2)}, u32[]{:S(2)}) collective-permute-start(f32[256,512]{1,0:T(8,128)S(1)} %bitcast.69), channel_id=1, source_target_pairs={{0,2},{2,0},{4,6},{6,4},{8,10},{10,8},{12,14},{14,12},{1,3},{3,1},... | collective-permute-start | bytes 1572872 | tf_op jit(solution)/shard_map/ppermute | solution.py:490
  344.9 14.4 %collective-permute-start.43 = (bf16[128,1024]{1,0:T(8,128)(2,1)S(1)}, bf16[128,1024]{1,0:T(8,128)(2,1)S(1)}, u32[]{:S(2)}, u32[]{:S(2)}) collective-permute-start(bf16[128,1024]{1,0:T(8,128)(2,1)S(1)} %copy-done.30), channel_id=1, source_target_pairs={{0,1},{1,0},{2,3},{3,2},{4,5},{5,4},{6,7},{7,6},{8,9},{9,8},{10,11... | collective-permute-start | bytes 786440 | tf_op jit(solution)/shard_map/ppermute | solution.py:459
  345.0 14.6 %collective-permute-start.44 = (bf16[128,1024]{1,0:T(8,128)(2,1)}, bf16[128,1024]{1,0:T(8,128)(2,1)S(1)}, u32[]{:S(2)}, u32[]{:S(2)}) collective-permute-start(bf16[128,1024]{1,0:T(8,128)(2,1)} %get-tuple-element.85), channel_id=1, source_target_pairs={{0,16},{16,0},{1,17},{17,1},{2,18},{18,2},{3,19},{19,3},{4,20},{20... | collective-permute-start | bytes 786440 | tf_op jit(solution)/shard_map/ppermute | solution.py:459
  345.9 13.8 %collective-permute-start.45 = (bf16[128,1024]{1,0:T(8,128)(2,1)}, bf16[128,1024]{1,0:T(8,128)(2,1)S(1)}, u32[]{:S(2)}, u32[]{:S(2)}) collective-permute-start(bf16[128,1024]{1,0:T(8,128)(2,1)} %get-tuple-element.86), channel_id=1, source_target_pairs={{0,17},{1,16},{16,1},{17,0},{2,19},{3,18},{18,3},{19,2},{4,21},{5,... | collective-permute-start | bytes 786440 | tf_op jit(solution)/shard_map/ppermute | solution.py:458
  346.8 14.1 %collective-permute-start.37 = (bf16[128,2048]{1,0:T(8,128)(2,1)}, bf16[128,2048]{1,0:T(8,128)(2,1)S(1)}, u32[]{:S(2)}, u32[]{:S(2)}) collective-permute-start(bf16[128,2048]{1,0:T(8,128)(2,1)} %get-tuple-element.76), channel_id=1, source_target_pairs={{0,1},{1,0},{2,3},{3,2},{4,5},{5,4},{6,7},{7,6},{8,9},{9,8},{10,11... | collective-permute-start | bytes 1572872 | tf_op jit(solution)/shard_map/ppermute | solution.py:459
  358.4 15.0 %collective-permute-start.38 = (bf16[128,2048]{1,0:T(8,128)(2,1)}, bf16[128,2048]{1,0:T(8,128)(2,1)S(1)}, u32[]{:S(2)}, u32[]{:S(2)}) collective-permute-start(bf16[128,2048]{1,0:T(8,128)(2,1)} %get-tuple-element.77), channel_id=1, source_target_pairs={{0,16},{16,0},{1,17},{17,1},{2,18},{18,2},{3,19},{19,3},{4,20},{20... | collective-permute-start | bytes 1572872 | tf_op jit(solution)/shard_map/ppermute | solution.py:459
  359.4 23.8 %collective-permute-start.39 = (bf16[128,2048]{1,0:T(8,128)(2,1)}, bf16[128,2048]{1,0:T(8,128)(2,1)}, u32[]{:S(2)}, u32[]{:S(2)}) collective-permute-start(bf16[128,2048]{1,0:T(8,128)(2,1)} %get-tuple-element.78), channel_id=1, source_target_pairs={{0,17},{1,16},{16,1},{17,0},{2,19},{3,18},{18,3},{19,2},{4,21},{5,... | collective-permute-start | bytes 1572872 | tf_op jit(solution)/shard_map/ppermute | solution.py:458
  359.6 9.0 %collective-permute-start.48 = (f32[128,512]{1,0:T(8,128)S(1)}, f32[128,512]{1,0:T(8,128)S(1)}, u32[]{:S(2)}, u32[]{:S(2)}) collective-permute-start(f32[128,512]{1,0:T(8,128)S(1)} %bitcast.70), channel_id=1, source_target_pairs={{0,4},{2,6},{4,0},{6,2},{8,12},{10,14},{12,8},{14,10},{1,5},{3,7},... | collective-permute-start | bytes 786440 | tf_op jit(solution)/shard_map/ppermute | solution.py:490
  359.7 24.6 %collective-permute-start.34 = (bf16[128,2048]{1,0:T(8,128)(2,1)}, bf16[128,2048]{1,0:T(8,128)(2,1)}, u32[]{:S(2)}, u32[]{:S(2)}) collective-permute-start(bf16[128,2048]{1,0:T(8,128)(2,1)} %get-tuple-element.72), channel_id=1, source_target_pairs={{0,1},{1,0},{2,3},{3,2},{4,5},{5,4},{6,7},{7,6},{8,9},{9,8},{10,11... | collective-permute-start | bytes 1572872 | tf_op jit(solution)/shard_map/ppermute | solution.py:459
  360.9 63.1 %collective-permute-start.40 = (bf16[128,2560]{1,0:T(8,128)(2,1)}, bf16[128,2560]{1,0:T(8,128)(2,1)S(1)}, u32[]{:S(2)}, u32[]{:S(2)}) collective-permute-start(bf16[128,2560]{1,0:T(8,128)(2,1)} %get-tuple-element.80), channel_id=1, source_target_pairs={{0,1},{1,0},{2,3},{3,2},{4,5},{5,4},{6,7},{7,6},{8,9},{9,8},{10,11... | collective-permute-start | bytes 1966088 | tf_op jit(solution)/shard_map/ppermute | solution.py:459
  368.6 56.5 %collective-permute-start.41 = (bf16[128,2560]{1,0:T(8,128)(2,1)}, bf16[128,2560]{1,0:T(8,128)(2,1)S(1)}, u32[]{:S(2)}, u32[]{:S(2)}) collective-permute-start(bf16[128,2560]{1,0:T(8,128)(2,1)} %get-tuple-element.81), channel_id=1, source_target_pairs={{0,16},{16,0},{1,17},{17,1},{2,18},{18,2},{3,19},{19,3},{4,20},{20... | collective-permute-start | bytes 1966088 | tf_op jit(solution)/shard_map/ppermute | solution.py:459
  373.4 52.7 %collective-permute-start.42 = (bf16[128,2560]{1,0:T(8,128)(2,1)}, bf16[128,2560]{1,0:T(8,128)(2,1)S(1)}, u32[]{:S(2)}, u32[]{:S(2)}) collective-permute-start(bf16[128,2560]{1,0:T(8,128)(2,1)} %get-tuple-element.82), channel_id=1, source_target_pairs={{0,17},{1,16},{16,1},{17,0},{2,19},{3,18},{18,3},{19,2},{4,21},{5,... | collective-permute-start | bytes 1966088 | tf_op jit(solution)/shard_map/ppermute | solution.py:458
  383.2 40.9 %collective-permute-start.35 = (bf16[128,2048]{1,0:T(8,128)(2,1)}, bf16[128,2048]{1,0:T(8,128)(2,1)}, u32[]{:S(2)}, u32[]{:S(2)}) collective-permute-start(bf16[128,2048]{1,0:T(8,128)(2,1)} %get-tuple-element.73), channel_id=1, source_target_pairs={{0,16},{16,0},{1,17},{17,1},{2,18},{18,2},{3,19},{19,3},{4,20},{20... | collective-permute-start | bytes 1572872 | tf_op jit(solution)/shard_map/ppermute | solution.py:459
  384.3 9.0 %collective-permute-start.49 = (f32[64,512]{1,0:T(8,128)S(1)}, f32[64,512]{1,0:T(8,128)S(1)}, u32[]{:S(2)}, u32[]{:S(2)}) collective-permute-start(f32[64,512]{1,0:T(8,128)S(1)} %dynamic-slice_bitcast_fusion.5), channel_id=1, source_target_pairs={{0,8},{2,10},{4,12},{6,14},{8,0},{10,2},{12,4},{14,6},{1,9},{3,11}... | collective-permute-start | bytes 393224 | tf_op jit(solution)/shard_map/ppermute | solution.py:490
  393.3 42.1 %collective-permute-start.36 = (bf16[128,2048]{1,0:T(8,128)(2,1)}, bf16[128,2048]{1,0:T(8,128)(2,1)}, u32[]{:S(2)}, u32[]{:S(2)}) collective-permute-start(bf16[128,2048]{1,0:T(8,128)(2,1)} %get-tuple-element.74), channel_id=1, source_target_pairs={{0,17},{1,16},{16,1},{17,0},{2,19},{3,18},{18,3},{19,2},{4,21},{5,... | collective-permute-start | bytes 1572872 | tf_op jit(solution)/shard_map/ppermute | solution.py:458
  424.0 14.2 %collective-permute-start.31 = (bf16[128,512]{1,0:T(8,128)(2,1)}, bf16[128,512]{1,0:T(8,128)(2,1)S(1)}, u32[]{:S(2)}, u32[]{:S(2)}) collective-permute-start(bf16[128,512]{1,0:T(8,128)(2,1)} %get-tuple-element.68), channel_id=1, source_target_pairs={{0,1},{1,0},{2,3},{3,2},{4,5},{5,4},{6,7},{7,6},{8,9},{9,8},{10,11... | collective-permute-start | bytes 393224 | tf_op jit(solution)/shard_map/ppermute | solution.py:459
  424.1 14.2 %collective-permute-start.32 = (bf16[128,512]{1,0:T(8,128)(2,1)}, bf16[128,512]{1,0:T(8,128)(2,1)S(1)}, u32[]{:S(2)}, u32[]{:S(2)}) collective-permute-start(bf16[128,512]{1,0:T(8,128)(2,1)} %get-tuple-element.69), channel_id=1, source_target_pairs={{0,16},{16,0},{1,17},{17,1},{2,18},{18,2},{3,19},{19,3},{4,20},{20... | collective-permute-start | bytes 393224 | tf_op jit(solution)/shard_map/ppermute | solution.py:459
  425.1 13.3 %collective-permute-start.33 = (bf16[128,512]{1,0:T(8,128)(2,1)}, bf16[128,512]{1,0:T(8,128)(2,1)}, u32[]{:S(2)}, u32[]{:S(2)}) collective-permute-start(bf16[128,512]{1,0:T(8,128)(2,1)} %get-tuple-element.70), channel_id=1, source_target_pairs={{0,17},{1,16},{16,1},{17,0},{2,19},{3,18},{18,3},{19,2},{4,21},{5,... | collective-permute-start | bytes 393224 | tf_op jit(solution)/shard_map/ppermute | solution.py:458
  426.1 14.8 %collective-permute-start.50 = (f32[64,256]{1,0:T(8,128)S(1)}, f32[64,256]{1,0:T(8,128)S(1)}, u32[]{:S(2)}, u32[]{:S(2)}) collective-permute-start(f32[64,256]{1,0:T(8,128)S(1)} %bitcast.71), channel_id=1, source_target_pairs={{0,16},{16,0},{1,17},{17,1},{2,18},{18,2},{3,19},{19,3},{4,20},{20... | collective-permute-start | bytes 196616 | tf_op jit(solution)/shard_map/ppermute | solution.py:459
  (51 other events, 459.7 us)
